TPU v7x, 32 devices: a whole 2x2x4 slice. The times are simulated.
32 devices in a mesh: group: 4 (over y, x), member: 8 (over z, core).
Axes of the slice: x: 2, y: 2, z: 4, core: 2. Of those that a mesh axis runs over, the one named last changes fastest.
Arguments:
- features: bfloat16 [131072, 128], P(('group', 'member')), may hold values from -6 to 6
- history: bfloat16 [131072, 128], P(('group', 'member')), may hold values from -6 to 6
- tiles: bfloat16 [16384, 128, 128], P(('group', 'member'))
- tile_src: int32 [1024, 16], P(('group', 'member')), may hold values from 0 to 47
- degree: int32 [131072], P(('group', 'member')), may hold values from 8 to 128
- boundary_rows: int32 [32, 256], P(('group', 'member')), may hold values from 0 to 4095
- picks: int32 [256, 1], P(('group', 'member')), may hold values from 0 to 1
- stale_rows: int32 [128, 256], P(('group', 'member')), may hold values from 0 to 4095
- w_self: bfloat16 [128, 128], replicated, may hold values from -0.5 to 0.5
- w_neigh: bfloat16 [128, 128], replicated, may hold values from -0.5 to 0.5
- cotangent: bfloat16 [131072, 128], P(('group', 'member')), may hold values from -6 to 6
Outputs:
- layer_out: bfloat16 [131072, 128], P(('group', 'member'))
- grad_features: bfloat16 [131072, 128], P(('group', 'member'))
- grad_self: float32 [128, 128], replicated
- grad_neigh: float32 [128, 128], replicated
Inputs may be any that keep to these rules, and one draw needn't show every extreme that they name: `boundary_rows`: local row indices of the sending device. `stale_rows`: local row indices of the sending device, one list for each destination group. `tile_src`: indices into the device's source blocks: own blocks, then taken boundary blocks member by member, then historical blocks group by group. `degree`: a normalizer given with the graph, not derived from the tiles.
All inputs are finite; a program needn't handle non-finite values.
Results may differ from a plain program's by a relative error of at most 0.0051.
Values may be sent and summed in bfloat16 or wider, within the bound.
A program may use at most 192 MiB of HBM per device.

v0:
```python
import math

import jax
import jax.numpy as jnp
from jax import lax
from jax.sharding import PartitionSpec as P


def on_device(
    features,
    history,
    tiles,
    tile_src,
    degree,
    boundary_rows,
    picks,
    stale_rows,
    w_self,
    w_neigh,
    cotangent,
):
    members = lax.axis_size("member")
    groups = lax.axis_size("group")
    tile = tiles.shape[1]
    width = features.shape[1]
    blocks = features.shape[0] // tile
    offered = boundary_rows.shape[1] // tile
    taken = picks.shape[1]
    bound = features[boundary_rows[0]].reshape(offered, tile, width)
    wanted = lax.all_to_all(picks, "member", split_axis=0, concat_axis=0, tiled=True)
    outgoing = bound[wanted]
    halo = lax.all_to_all(outgoing, "member", split_axis=0, concat_axis=0, tiled=True)
    stale = lax.all_to_all(
        history[stale_rows], "group", split_axis=0, concat_axis=0, tiled=True
    ).reshape(-1, tile, width)
    sources = jnp.concatenate(
        [features.reshape(blocks, tile, width), halo.reshape(-1, tile, width), stale], axis=0
    )
    tiled = tiles.reshape(blocks, -1, tile, tile)
    picked = sources[tile_src]
    summed = jnp.einsum("btij,btjf->bif", tiled, picked, preferred_element_type=jnp.float32)
    degs = degree.astype(jnp.float32)[:, None]
    agg = (summed.reshape(-1, width) / degs).astype(jnp.bfloat16)
    pre = jnp.dot(features, w_self, preferred_element_type=jnp.float32) + jnp.dot(
        agg, w_neigh, preferred_element_type=jnp.float32
    )
    scale_row = lax.rsqrt(jnp.mean(pre * pre, axis=-1, keepdims=True) + 1e-05)
    layer_out = (pre * scale_row).astype(jnp.bfloat16)
    grad_out = cotangent.astype(jnp.float32)
    dpre = (
        scale_row * grad_out - pre * scale_row**3 * jnp.mean(grad_out * pre, axis=-1, keepdims=True)
    ).astype(jnp.bfloat16)
    part_self = jnp.dot(features.T, dpre, preferred_element_type=jnp.float32)
    part_neigh = jnp.dot(agg.T, dpre, preferred_element_type=jnp.float32)
    dself = jnp.dot(dpre, w_self.T, preferred_element_type=jnp.float32)
    back = (jnp.dot(dpre, w_neigh.T, preferred_element_type=jnp.float32) / degs).astype(
        jnp.bfloat16
    )
    back = back.reshape(blocks, tile, width)
    per_tile = jnp.einsum("btij,bif->btjf", tiled, back, preferred_element_type=jnp.float32)
    count_sources = sources.shape[0]
    onehot = (
        tile_src[:, :, None] == jnp.arange(count_sources, dtype=jnp.int32)[None, None, :]
    ).astype(jnp.float32)
    src_grad = jnp.einsum(
        "bts,btjf->sjf",
        onehot,
        per_tile,
        precision=lax.Precision.HIGHEST,
        preferred_element_type=jnp.float32,
    )
    local_grad = src_grad[:blocks].reshape(-1, width)
    halo_grad = src_grad[blocks : blocks + members * taken].reshape(members, taken, tile, width)
    returned = lax.all_to_all(
        halo_grad.astype(jnp.bfloat16), "member", split_axis=0, concat_axis=0, tiled=True
    ).astype(halo_grad.dtype)
    bound_grad = jnp.zeros((offered, tile, width), jnp.float32).at[wanted].add(returned)
    row_grad = dself + local_grad
    row_grad = row_grad.at[boundary_rows[0]].add(bound_grad.reshape(-1, width))
    grad_features = row_grad.astype(jnp.bfloat16)
    share_self, share_neigh = (
        lax.psum_scatter(part_self, "member", scatter_dimension=0, tiled=True),
        lax.psum_scatter(part_neigh, "member", scatter_dimension=0, tiled=True),
    )
    share_self, share_neigh = lax.psum((share_self, share_neigh), "group")
    grad_self, grad_neigh = (
        lax.all_gather(share_self, "member", axis=0, tiled=True),
        lax.all_gather(share_neigh, "member", axis=0, tiled=True),
    )
    factor = 1.0 / math.sqrt(features.shape[0] * members * groups)
    return (layer_out, grad_features, grad_self * factor, grad_neigh * factor)


def solution(mesh):
    placed = (
        P(("group", "member"), None),
        P(("group", "member"), None),
        P(("group", "member"), None, None),
        P(("group", "member"), None),
        P(("group", "member")),
        P(("group", "member"), None),
        P(("group", "member"), None),
        P(("group", "member"), None),
        P(),
        P(),
        P(("group", "member"), None),
    )
    return jax.shard_map(
        on_device,
        mesh=mesh,
        in_specs=placed,
        out_specs=(P(("group", "member"), None), P(("group", "member"), None), P(), P()),
        check_vma=False,
    )
```

profile of v0, /device:TPU:0, one launch (start us, length us, event | category | flops | bytes accessed | tf_op | source)
XLA Modules:
  0.0 253.7 jit_solution(7112376655668835784)
XLA Ops:
  7.2 1.4 copy.40
  8.6 6.4 %all-to-all-start = ((s32[8,1,1]{2,1,0:T(1,128)}), s32[8,1,1]{2,1,0:T(1,128)S(1)}, u32[]{:S(2)}, u32[]{:S(2)}) async-start(s32[8,1,1]{2,1,0:T(1,128)} %copy.40), calls=%async_computation | async-start | bytes 8192 | tf_op jit(solution)/shard_map/all_to_all | solution.py:30
  16.3 2.1 gather_fusion
  18.5 4.3 %gather_fusion.2 = bf16[1024,128]{1,0:T(8,128)(2,1)} fusion(bf16[4096,128]{1,0:T(8,128)(2,1)S(1)} %copy-done, s32[1024]{0:T(1024)S(1)} %broadcast_clamp_fusion), kind=kCustom, calls=%fused_computation.2 | custom fusion | bytes 528384 | tf_op jit(solution)/shard_map/gather | solution.py:34
  22.8 3.9 %all-to-all-start.2 = ((bf16[4,256,128]{2,1,0:T(8,128)(2,1)}), bf16[4,256,128]{2,1,0:T(8,128)(2,1)S(1)}, u32[]{:S(2)}, u32[]{:S(2)}) async-start(bf16[4,256,128]{2,1,0:T(8,128)(2,1)} %bitcast.7), calls=%async_computation.2 | async-start | bytes 524288 | tf_op jit(solution)/shard_map/all_to_all | solution.py:33
  28.2 4.5 %all-to-all-done.2 = bf16[4,256,128]{2,1,0:T(8,128)(2,1)S(1)} async-done(((bf16[4,256,128]{2,1,0:T(8,128)(2,1)}), bf16[4,256,128]{2,1,0:T(8,128)(2,1)S(1)}, u32[]{:S(2)}, u32[]{:S(2)}) %all-to-all-start.2) | async-done | bytes 262176 | tf_op jit(solution)/shard_map/all_to_all | solution.py:33
  32.7 4.7 %all-to-all-start.1 = ((bf16[8,1,128,128]{3,2,1,0:T(8,128)(2,1)}), bf16[8,1,128,128]{3,2,1,0:T(8,128)(2,1)S(1)}, u32[]{:S(2)}, u32[]{:S(2)}) async-start(bf16[8,1,128,128]{3,2,1,0:T(8,128)(2,1)} %bitcast.5), calls=%async_computation.1 | async-start | bytes 524288 | tf_op jit(solution)/shard_map/all_to_all | solution.py:32
  37.6 1.3 copy.42
  39.0 1.8 fusion.11
  40.8 6.3 %all-to-all-done.1 = bf16[8,1,128,128]{3,2,1,0:T(8,128)(2,1)S(1)} async-done(((bf16[8,1,128,128]{3,2,1,0:T(8,128)(2,1)}), bf16[8,1,128,128]{3,2,1,0:T(8,128)(2,1)S(1)}, u32[]{:S(2)}, u32[]{:S(2)}) %all-to-all-start.1) | async-done | bytes 262176 | tf_op jit(solution)/shard_map/all_to_all | solution.py:32
  47.3 13.9 %gather_fusion.3 = bf16[512,128,128]{2,1,0:T(8,128)(2,1)} fusion(bf16[48,128,128]{2,1,0:T(8,128)(2,1)S(1)} %pad_maximum_fusion, s32[1024]{0:T(1024)S(1)} %pad_clamp_fusion), kind=kCustom, calls=%fused_computation.3 | custom fusion | bytes 33556480 | tf_op jit(solution)/shard_map/gather | solution.py:40
  61.2 15.1 %fusion.12 = f32[32,128,128,1]{1,2,3,0:T(8,128)S(1)} fusion(bf16[32,16,128,128]{3,2,1,0:T(8,128)(2,1)} %bitcast.65, bf16[32,16,128,128]{3,2,1,0:T(8,128)(2,1)} %bitcast.67), kind=kOutput, calls=%fused_computation.45 | convolution fusion | flops 2147483648 | bytes 35651584 | tf_op jit(solution)/shard_map/btij,btjf->bif/dot_general | solution.py:41
  79.0 1.5 fusion.2
  82.9 21.5 %convolution_bitcast_fusion = f32[32,16,128,128]{2,3,1,0:T(8,128)} fusion(bf16[32,128,128,1]{2,1,3,0:T(8,128)(2,1)S(1)} %bitcast.71, bf16[32,16,128,128]{3,2,1,0:T(8,128)(2,1)} %bitcast.66), kind=kOutput, calls=%fused_computation.6 | convolution fusion | flops 2147483648 | bytes 51380224 | tf_op jit(solution)/shard_map/btij,bif->btjf/dot_general | solution.py:60
  104.4 34.6 %copy.44 = f32[32,16,128,128]{3,0,1,2:T(8,128)} copy(f32[32,16,128,128]{2,3,1,0:T(8,128)} %convolution_bitcast_fusion) | data formatting | bytes 67108864 | tf_op jit(solution)/shard_map/btij,bif->btjf/dot_general | solution.py:60
  138.9 18.5 %convolution_bitcast_fusion.1 = f32[48,128,128]{2,0,1:T(8,128)} fusion(f32[32,16,128,128]{3,0,1,2:T(8,128)} %copy.44, s32[32,16]{0,1:T(8,128)S(1)} %copy-done.9), kind=kOutput, calls=%fused_computation.20 | convolution fusion | flops 4831862784 | bytes 36702208 | tf_op jit(solution)/shard_map/bts,btjf->sjf/dot_general | solution.py:65
  157.4 1.6 slice-done
  161.9 2.3 copy.50
  166.7 3.4 %all-to-all-start.3 = ((bf16[8,1,128,128]{3,2,1,0:T(8,128)(2,1)}), bf16[8,1,128,128]{3,2,1,0:T(8,128)(2,1)S(1)}, u32[]{:S(2)}, u32[]{:S(2)}) async-start(bf16[8,1,128,128]{3,2,1,0:T(8,128)(2,1)} %copy.46), calls=%async_computation.3 | async-start | bytes 524288 | tf_op jit(solution)/shard_map/all_to_all | solution.py:74
  171.0 22.4 %reduce-scatter.7.cloned.1.call-done = f32[16,128]{1,0:T(8,128)} async-done(((f32[128,128]{1,0:T(8,128)}), f32[16,128]{1,0:T(8,128)}) %reduce-scatter.7.cloned.1.call-update) | async-done | bytes 8208
  194.2 18.2 %all-reduce = (f32[16,128]{0,1:T(8,128)S(1)}, f32[16,128]{0,1:T(8,128)S(1)}) all-reduce(f32[16,128]{0,1:T(8,128)S(1)} %copy.58, f32[16,128]{0,1:T(8,128)S(1)} %copy.60), channel_id=1, replica_groups=mesh['group'=4,'member'=8] {'group'}, use_global_device_ids=true, to_apply=%region_5.0 | all-reduce | flops 4096 | bytes 32768 | tf_op jit(solution)/shard_map/psum | solution.py:85
  212.5 14.0 %all_gather.7 = f32[128,128]{1,0:T(8,128)S(1)} all-gather(f32[16,128]{1,0:T(8,128)S(1)} %copy.49), channel_id=1, replica_groups=mesh['group'=4,'member'=8] {'member'}, dimensions={0}, use_global_device_ids=true | all-gather | bytes 73728 | tf_op jit(solution)/shard_map/all_gather | solution.py:88
  226.5 14.2 %all_gather.6 = f32[128,128]{1,0:T(8,128)S(1)} all-gather(f32[16,128]{1,0:T(8,128)S(1)} %copy.47), channel_id=1, replica_groups=mesh['group'=4,'member'=8] {'member'}, dimensions={0}, use_global_device_ids=true | all-gather | bytes 73728 | tf_op jit(solution)/shard_map/all_gather | solution.py:87
  243.1 2.7 %scatter_fusion.1 = f32[4096,128]{1,0:T(8,128)S(1)} fusion(f32[4096,128]{1,0:T(8,128)S(1)} %convolution_add_fusion, s32[256]{0:T(256)S(1)} %bitcast.77, f32[256,128]{1,0:T(8,128)S(1)} %bitcast.70), kind=kCustom, calls=%fused_computation.5 | custom fusion | flops 32768 | bytes 394240 | tf_op jit(solution)/shard_map/scatter-add | solution.py:79
  (65 shorter events, 19.0 us)
Async XLA Ops:
  7.2 11.3 %copy-start = (bf16[4096,128]{1,0:T(8,128)(2,1)S(1)}, bf16[4096,128]{1,0:T(8,128)(2,1)}, u32[]{:S(2)}) copy-start(bf16[4096,128]{1,0:T(8,128)(2,1)} %param.12) | copy-start | bytes 3145732
  8.6 14.2 %all-to-all-start = ((s32[8,1,1]{2,1,0:T(1,128)}), s32[8,1,1]{2,1,0:T(1,128)S(1)}, u32[]{:S(2)}, u32[]{:S(2)}) async-start(s32[8,1,1]{2,1,0:T(1,128)} %copy.40), calls=%async_computation | async-start | bytes 8192 | tf_op jit(solution)/shard_map/all_to_all | solution.py:30
  18.4 19.0 %copy-start.9 = (s32[32,16]{0,1:T(8,128)S(1)}, s32[32,16]{0,1:T(8,128)}, u32[]{:S(2)}) copy-start(s32[32,16]{0,1:T(8,128)} %param.14) | copy-start | bytes 6148
  18.4 19.2 %copy-start.10 = (s32[4096]{0:T(1024)S(1)}, s32[4096]{0:T(1024)}, u32[]{:S(2)}) copy-start(s32[4096]{0:T(1024)} %param.15) | copy-start | bytes 49156
  18.5 19.2 %copy-start.6 = (bf16[4096,128]{1,0:T(8,128)(2,1)S(1)}, bf16[4096,128]{1,0:T(8,128)(2,1)}, u32[]{:S(2)}) copy-start(bf16[4096,128]{1,0:T(8,128)(2,1)} %param.21) | copy-start | bytes 3145732
  22.8 16.2 %copy-start.2 = (bf16[4096,128]{1,0:T(8,128)(2,1)S(1)}, bf16[4096,128]{1,0:T(8,128)(2,1)}, u32[]{:S(2)}) copy-start(bf16[4096,128]{1,0:T(8,128)(2,1)} %param.11) | copy-start | bytes 3145732
  22.8 16.2 %copy-start.7 = (bf16[128,128]{1,0:T(8,128)(2,1)S(1)}, bf16[128,128]{1,0:T(8,128)(2,1)}, u32[]{:S(2)}) copy-start(bf16[128,128]{1,0:T(8,128)(2,1)} %param.19) | copy-start | bytes 98308
  22.8 9.9 %all-to-all-start.2 = ((bf16[4,256,128]{2,1,0:T(8,128)(2,1)}), bf16[4,256,128]{2,1,0:T(8,128)(2,1)S(1)}, u32[]{:S(2)}, u32[]{:S(2)}) async-start(bf16[4,256,128]{2,1,0:T(8,128)(2,1)} %bitcast.7), calls=%async_computation.2 | async-start | bytes 524288 | tf_op jit(solution)/shard_map/all_to_all | solution.py:33
  32.7 14.4 %all-to-all-start.1 = ((bf16[8,1,128,128]{3,2,1,0:T(8,128)(2,1)}), bf16[8,1,128,128]{3,2,1,0:T(8,128)(2,1)S(1)}, u32[]{:S(2)}, u32[]{:S(2)}) async-start(bf16[8,1,128,128]{3,2,1,0:T(8,128)(2,1)} %bitcast.5), calls=%async_computation.1 | async-start | bytes 524288 | tf_op jit(solution)/shard_map/all_to_all | solution.py:32
  37.4 132.8 %reduce-scatter.9.cloned.1.call-start = ((), (), s32[]{:S(2)}) async-start(), calls=%async_computation.7 | async-start | bytes 73728
  61.2 16.0 %copy-start.8 = (bf16[128,128]{1,0:T(8,128)(2,1)S(1)}, bf16[128,128]{1,0:T(8,128)(2,1)}, u32[]{:S(2)}) copy-start(bf16[128,128]{1,0:T(8,128)(2,1)} %param.20) | copy-start | bytes 98308
  76.3 1.2 copy-start.4
  76.3 1.9 copy-start.5
  82.7 110.7 %reduce-scatter.7.cloned.1.call-start = ((), (), s32[]{:S(2)}) async-start(), calls=%async_computation.6 | async-start | bytes 73728
  157.4 1.6 slice-start
  160.2 1.2 copy-start.3
  166.7 75.3 %all-to-all-start.3 = ((bf16[8,1,128,128]{3,2,1,0:T(8,128)(2,1)}), bf16[8,1,128,128]{3,2,1,0:T(8,128)(2,1)S(1)}, u32[]{:S(2)}, u32[]{:S(2)}) async-start(bf16[8,1,128,128]{3,2,1,0:T(8,128)(2,1)} %copy.46), calls=%async_computation.3 | async-start | bytes 524288 | tf_op jit(solution)/shard_map/all_to_all | solution.py:74
  243.1 3.8 %copy-start.1 = (bf16[4096,128]{1,0:T(8,128)(2,1)S(1)}, bf16[4096,128]{1,0:T(8,128)(2,1)}, u32[]{:S(2)}) copy-start(bf16[4096,128]{1,0:T(8,128)(2,1)} %param.12) | copy-start | bytes 3145732
Sparse Core Ops, SparseCore 0:
  82.8 28.2 reduce-scatter.8
  165.0 28.2 reduce-scatter.6
where the time goes:
time: 255 us; the launch traced here: 254 us
  local copies, waits for them, and re-layouts  70.1 us (27%)
  matrix products  60.7 us (24%)
  blocking collectives  46.4 us (18%)
  waiting for transfers between devices  33.3 us (13%)
  starting transfers between devices  18.6 us (7%)
  between operations  14.3 us (6%)
  other arithmetic  10.3 us (4%)
    dot_general x1, local copies, waits for them, and re-layouts, on_device(): jnp.einsum('btij,bif->btjf', tiled, back, preferred_element_type=jnp.floa...  34.6 us
    unnamed x4, waiting for transfers between devices  22.5 us
    dot_general x1, matrix products, on_device(): jnp.einsum('btij,bif->btjf', tiled, back, preferred_element_type=jnp.floa...  21.5 us
    dot_general x1, matrix products, on_device(): jnp.einsum('bts,btjf->sjf', onehot, per_tile, precision=lax.Precision.HIG...  18.5 us
    psum x1, blocking collectives, on_device(): share_self, share_neigh = lax.psum((share_self, share_neigh), 'group')  18.2 us
    dot_general x1, matrix products, on_device(): jnp.einsum('btij,btjf->bif', tiled, picked, preferred_element_type=jnp.fl...  15.1 us
    all_gather x1, blocking collectives, on_device(): lax.all_gather(share_self, 'member', axis=0, tiled=True)  14.2 us
    all_gather x1, blocking collectives, on_device(): lax.all_gather(share_neigh, 'member', axis=0, tiled=True)  14 us
  transfers between devices with their start and end apart: 6, of which 3 were waited for; matrix products, arithmetic and copies ran while one was open for 38% of the time, Pallas kernels for 0%

commit v1 on v0

v1 whole, which is shorter than its diff:
```python
import functools
import math

import jax
import jax.numpy as jnp
from jax import lax
from jax.experimental import pallas as pl
from jax.experimental.pallas import tpu as pltpu
from jax.sharding import PartitionSpec as P

QUAD = 4
F32 = jnp.float32
BF16 = jnp.bfloat16


def plan(tile_src, wanted_sources):
    flat = tile_src.reshape(-1)
    total = flat.shape[0]
    slots = (total + wanted_sources * (QUAD - 1)) // QUAD * QUAD
    index = jnp.arange(total, dtype=jnp.int32)
    same = flat[:, None] == flat[None, :]
    within = jnp.sum(jnp.where(same & (index[None, :] < index[:, None]), 1, 0), axis=1)
    ids = jnp.arange(wanted_sources, dtype=jnp.int32)
    hit = flat[None, :] == ids[:, None]
    count = jnp.sum(hit.astype(jnp.int32), axis=1)
    padded = (count + QUAD - 1) // QUAD * QUAD
    offset = jnp.sum(jnp.where(ids[None, :] < ids[:, None], padded[None, :], 0), axis=1)
    base = jnp.sum(jnp.where(hit, offset[:, None], 0), axis=0)
    pos = jnp.where(flat < wanted_sources, base + within, -1)
    slot = jnp.arange(slots, dtype=jnp.int32)
    code = jnp.sum(jnp.where(pos[None, :] == slot[:, None], index[None, :] + 1, 0), axis=1)
    first = slot[::QUAD]
    inside = (offset[None, :] <= first[:, None]) & (first[:, None] < (offset + padded)[None, :])
    start = inside & (offset[None, :] == first[:, None])
    quad = jnp.sum(jnp.where(inside, 2 * ids[None, :], 0) + start.astype(jnp.int32), axis=1)
    used = (jnp.sum(padded) // QUAD).reshape(1)
    return code, quad, used


def local_kernel(
    src,
    code,
    quad,
    used,
    feats,
    halo,
    stale,
    tiles,
    deg,
    w_self,
    w_neigh,
    cot,
    out,
    row_grad,
    halo_grad,
    g_self,
    g_neigh,
    tbuf,
    srcs,
    agg,
    back,
    grad,
    gt,
    sems,
):
    blocks, per = src.shape
    tile, width = feats.shape[0] // blocks, feats.shape[1]
    n_halo, n_stale = halo.shape[0], stale.shape[0]

    def chunk(b):
        return pltpu.make_async_copy(
            tiles.at[pl.ds(b * per, per)], tbuf.at[pl.ds(b * per, per)], sems.at[b]
        )

    @pl.loop(0, blocks)
    def _(b):
        chunk(b).start()

    for b in range(blocks):
        srcs[b] = feats[b * tile : (b + 1) * tile, :]
    srcs[blocks : blocks + n_halo] = halo[...]
    srcs[blocks + n_halo :] = stale[...]
    grad[...] = jnp.zeros_like(grad)
    back[blocks] = jnp.zeros((width, tile), BF16)

    def forward(b):
        chunk(b).wait()
        lhs = jnp.concatenate([tbuf[b * per + t] for t in range(per)], axis=1)
        rhs = jnp.concatenate([srcs[src[b, t]] for t in range(per)], axis=0)
        total = jnp.dot(lhs, rhs, preferred_element_type=F32)
        d = jnp.broadcast_to(deg[pl.ds(b, 1), :].astype(F32), (tile, tile)).T
        agg[pl.ds(pl.multiple_of(b * tile, tile), tile), :] = (total / d).astype(BF16)

    pl.loop(0, blocks, unroll=2)(forward)

    gt[...] = jnp.zeros_like(gt)
    group = 4
    rows = group * tile
    w_cat = jnp.concatenate([w_self[...], w_neigh[...]], axis=0)

    def middle(c):
        at = pl.ds(pl.multiple_of(c * rows, rows), rows)
        fa = jnp.concatenate([feats[at, :], agg[at, :]], axis=1)
        pre = jnp.dot(fa, w_cat, preferred_element_type=F32)
        scale = lax.rsqrt(jnp.mean(pre * pre, axis=-1, keepdims=True) + 1e-05)
        out[at, :] = (pre * scale).astype(BF16)
        g = cot[at, :].astype(F32)
        m = jnp.mean(g * pre, axis=-1, keepdims=True)
        dpre = (scale * g - pre * (scale**3 * m)).astype(BF16)
        gt[...] += lax.dot_general(dpre, fa, (((0,), (0,)), ((), ())), preferred_element_type=F32)
        row_grad[at, :] = lax.dot_general(
            dpre, w_self[...], (((1,), (1,)), ((), ())), preferred_element_type=F32
        )
        bt = lax.dot_general(
            w_neigh[...], dpre, (((1,), (1,)), ((), ())), preferred_element_type=F32
        )
        for i in range(group):
            d = deg[pl.ds(c * group + i, 1), :].astype(F32)
            back[c * group + i] = (bt[:, i * tile : (i + 1) * tile] / d).astype(BF16)

    pl.loop(0, blocks // group)(middle)

    g_self[...] = gt[:, :width].T
    g_neigh[...] = gt[:, width:].T

    def backward(q, acc):
        lhs, rhs = [], []
        for i in range(QUAD):
            k = code[q * QUAD + i]
            t = jnp.maximum(k - 1, 0)
            b = jnp.where(k == 0, blocks, t // per)
            lhs.append(back[b])
            rhs.append(tbuf[t])
        term = jnp.dot(
            jnp.concatenate(lhs, axis=1),
            jnp.concatenate(rhs, axis=0),
            preferred_element_type=F32,
        )
        info = quad[q]
        acc = term + jnp.where(info % 2 == 1, 0.0, acc)
        grad[info // 2] = acc
        return acc

    lax.fori_loop(0, used[0], backward, jnp.zeros((width, tile), F32))

    def finish(b):
        at = pl.ds(pl.multiple_of(b * tile, tile), tile)
        row_grad[at, :] += grad[b].T

    pl.loop(0, blocks, unroll=4)(finish)
    for h in range(n_halo):
        halo_grad[h] = grad[blocks + h].T.astype(BF16)


def local(tile_src, plans, features, halo, stale, tiles, degree, w_self, w_neigh, cotangent):
    blocks, per = tile_src.shape
    tile = tiles.shape[1]
    nodes, width = features.shape
    n_halo = halo.shape[0]
    smem = pl.BlockSpec(memory_space=pltpu.SMEM)
    vmem = pl.BlockSpec(memory_space=pltpu.VMEM)
    return pl.pallas_call(
        local_kernel,
        out_shape=(
            jax.ShapeDtypeStruct((nodes, width), BF16),
            jax.ShapeDtypeStruct((nodes, width), F32),
            jax.ShapeDtypeStruct((n_halo, tile, width), BF16),
            jax.ShapeDtypeStruct((width, width), F32),
            jax.ShapeDtypeStruct((width, width), F32),
        ),
        in_specs=[smem] * 4
        + [vmem] * 3
        + [pl.BlockSpec(memory_space=pl.ANY)]
        + [vmem] * 4,
        out_specs=[vmem] * 5,
        scratch_shapes=[
            pltpu.VMEM(tiles.shape, BF16),
            pltpu.VMEM((blocks + n_halo + stale.shape[0], tile, width), BF16),
            pltpu.VMEM((nodes, width), BF16),
            pltpu.VMEM((blocks + 1, width, tile), BF16),
            pltpu.VMEM((blocks + n_halo, width, tile), F32),
            pltpu.VMEM((width, 2 * width), F32),
            pltpu.SemaphoreType.DMA((blocks,)),
        ],
        compiler_params=pltpu.CompilerParams(vmem_limit_bytes=60 << 20),
    )(
        tile_src,
        *plans,
        features,
        halo,
        stale,
        tiles,
        degree.reshape(blocks, tile),
        w_self,
        w_neigh,
        cotangent,
    )


def on_device(
    features,
    history,
    tiles,
    tile_src,
    degree,
    boundary_rows,
    picks,
    stale_rows,
    w_self,
    w_neigh,
    cotangent,
):
    members = lax.axis_size("member")
    groups = lax.axis_size("group")
    tile = tiles.shape[1]
    width = features.shape[1]
    blocks = features.shape[0] // tile
    offered = boundary_rows.shape[1] // tile
    taken = picks.shape[1]
    bound = features[boundary_rows[0]].reshape(offered, tile, width)
    wanted = lax.all_to_all(picks, "member", split_axis=0, concat_axis=0, tiled=True)
    outgoing = bound[wanted]
    halo = lax.all_to_all(outgoing, "member", split_axis=0, concat_axis=0, tiled=True)
    stale = lax.all_to_all(
        history[stale_rows], "group", split_axis=0, concat_axis=0, tiled=True
    ).reshape(-1, tile, width)
    plans = plan(tile_src, blocks + members * taken)
    layer_out, row_grad, halo_grad, part_self, part_neigh = local(
        tile_src,
        plans,
        features,
        halo.reshape(-1, tile, width),
        stale,
        tiles,
        degree,
        w_self,
        w_neigh,
        cotangent,
    )
    returned = lax.all_to_all(
        halo_grad.reshape(members, taken, tile, width),
        "member",
        split_axis=0,
        concat_axis=0,
        tiled=True,
    ).astype(F32)
    bound_grad = jnp.zeros((offered, tile, width), F32).at[wanted].add(returned)
    row_grad = row_grad.at[boundary_rows[0]].add(bound_grad.reshape(-1, width))
    grad_features = row_grad.astype(BF16)
    parts = jnp.concatenate([part_self, part_neigh], axis=0)
    share = lax.psum_scatter(parts, "member", scatter_dimension=0, tiled=True)
    share = lax.psum(share, "group")
    whole = lax.all_gather(share, "member", axis=0, tiled=True)
    factor = 1.0 / math.sqrt(features.shape[0] * members * groups)
    return (layer_out, grad_features, whole[:width] * factor, whole[width:] * factor)


def solution(mesh):
    placed = (
        P(("group", "member"), None),
        P(("group", "member"), None),
        P(("group", "member"), None, None),
        P(("group", "member"), None),
        P(("group", "member")),
        P(("group", "member"), None),
        P(("group", "member"), None),
        P(("group", "member"), None),
        P(),
        P(),
        P(("group", "member"), None),
    )
    return jax.shard_map(
        on_device,
        mesh=mesh,
        in_specs=placed,
        out_specs=(P(("group", "member"), None), P(("group", "member"), None), P(), P()),
        check_vma=False,
    )
```

time: 255 us -> 173 us (0.68)
  matrix products: 60.7 us -> 0 us
  local copies, waits for them, and re-layouts: 70.1 us -> 10.9 us
  Pallas kernels: 0 us -> 43.7 us
  blocking collectives: 46.4 us -> 30.5 us
  waiting for transfers between devices: 33.3 us -> 38.3 us
  other arithmetic: 10.3 us -> 13.4 us
    dot_general x8 -> x0, matrix products: 59.5 us -> none  [the longest x1 21.5 us: on_device(): jnp.einsum('btij,bif->btjf', tiled, back, preferred_element_type=jnp.floa...]
    pallas_call x0 -> x1, Pallas kernels: none -> 43.7 us  [local(): pl.pallas_call(local_kernel, out_shape=(jax.ShapeDtypeStruct((nodes, widt...]
    dot_general x1 -> x0, local copies, waits for them, and re-layouts: 34.6 us -> none  [on_device(): jnp.einsum('btij,bif->btjf', tiled, back, preferred_element_type=jnp.floa...]
    reduce_scatter x0 -> x1, waiting for transfers between devices: none -> 25 us  [on_device(): share = lax.psum_scatter(parts, 'member', scatter_dimension=0, tiled=True)]
    unnamed x4 -> x1, waiting for transfers between devices: 22.5 us -> 0.02 us
    all_gather x2 -> x1, blocking collectives: 28.2 us -> 13.9 us  [on_device(): whole = lax.all_gather(share, 'member', axis=0, tiled=True)]
    gather x1 -> x0, local copies, waits for them, and re-layouts: 13.9 us -> none  [on_device(): picked = sources[tile_src]]
    unnamed x28 -> x12, local copies, waits for them, and re-layouts: 7.67 us -> 1.5 us
  transfers between devices with their start and end apart: 6 -> 5, of which waited for: 3 -> 3; matrix products, arithmetic and copies ran while one was open for 38% -> 8% of each run, Pallas kernels for 0% -> 0%
where the time goes in v1:
time: 173 us; the launch traced here: 172 us
  Pallas kernels  43.7 us (25%)
  waiting for transfers between devices  38.3 us (22%)
  blocking collectives  30.5 us (18%)
  starting transfers between devices  18.2 us (11%)
  between operations  16.7 us (10%)
  other arithmetic  13.4 us (8%)
  local copies, waits for them, and re-layouts  10.9 us (6%)
    pallas_call x1, Pallas kernels, local(): pl.pallas_call(local_kernel, out_shape=(jax.ShapeDtypeStruct((nodes, widt...  43.7 us
    reduce_scatter x1, waiting for transfers between devices, on_device(): share = lax.psum_scatter(parts, 'member', scatter_dimension=0, tiled=True)  25 us
    psum x1, blocking collectives, on_device(): share = lax.psum(share, 'group')  16.5 us
    all_gather x1, blocking collectives, on_device(): whole = lax.all_gather(share, 'member', axis=0, tiled=True)  13.9 us
    all_to_all x1, waiting for transfers between devices, on_device(): lax.all_to_all(outgoing, 'member', split_axis=0, concat_axis=0, tiled=True)  8.76 us
    all_to_all x1, starting transfers between devices, on_device(): lax.all_to_all(picks, 'member', split_axis=0, concat_axis=0, tiled=True)  6.35 us
    all_to_all x1, starting transfers between devices, on_device(): lax.all_to_all(outgoing, 'member', split_axis=0, concat_axis=0, tiled=True)  4.71 us
    all_to_all x1, waiting for transfers between devices, on_device(): lax.all_to_all(history[stale_rows], 'group', split_axis=0, concat_axis=0,...  4.49 us
  transfers between devices with their start and end apart: 5, of which 3 were waited for; matrix products, arithmetic and copies ran while one was open for 8% of the time, Pallas kernels for 0%

profile of v1, /device:TPU:0, one launch (start us, length us, event | category | flops | bytes accessed | tf_op | source)
XLA Modules:
  0.0 171.7 jit_solution(6001118675436086058)
XLA Ops:
  7.2 1.4 copy.27
  8.6 6.4 %all-to-all-start = ((s32[8,1,1]{2,1,0:T(1,128)}), s32[8,1,1]{2,1,0:T(1,128)S(1)}, u32[]{:S(2)}, u32[]{:S(2)}) async-start(s32[8,1,1]{2,1,0:T(1,128)} %copy.27), calls=%async_computation | async-start | bytes 8192 | tf_op jit(solution)/shard_map/all_to_all | solution.py:221
  14.9 0.8 copy.28.src
  18.8 0.7 fusion.1
  21.2 2.1 %gather_fusion = bf16[256,128]{1,0:T(8,128)(2,1)S(1)} fusion(bf16[4096,128]{1,0:T(8,128)(2,1)} %feats.1, s32[1024]{0:T(1024)S(1)} %pad_clamp_fusion.1), kind=kCustom, calls=%fused_computation | custom fusion | bytes 132096 | tf_op jit(solution)/shard_map/gather | solution.py:220
  23.3 0.7 add_reduce_fusion.quad
  24.0 4.3 %gather_fusion.2 = bf16[1024,128]{1,0:T(8,128)(2,1)} fusion(bf16[4096,128]{1,0:T(8,128)(2,1)S(1)} %copy-done, s32[1024]{0:T(1024)S(1)} %broadcast_clamp_fusion), kind=kCustom, calls=%fused_computation.2 | custom fusion | bytes 528384 | tf_op jit(solution)/shard_map/gather | solution.py:225
  28.3 3.7 %all-to-all-start.2 = ((bf16[4,256,128]{2,1,0:T(8,128)(2,1)}), bf16[4,256,128]{2,1,0:T(8,128)(2,1)S(1)}, u32[]{:S(2)}, u32[]{:S(2)}) async-start(bf16[4,256,128]{2,1,0:T(8,128)(2,1)} %bitcast.7), calls=%async_computation.2 | async-start | bytes 524288 | tf_op jit(solution)/shard_map/all_to_all | solution.py:224
  32.3 1.3 gather_fusion.1
  33.6 4.5 %all-to-all-done.2 = bf16[4,256,128]{2,1,0:T(8,128)(2,1)S(1)} async-done(((bf16[4,256,128]{2,1,0:T(8,128)(2,1)}), bf16[4,256,128]{2,1,0:T(8,128)(2,1)S(1)}, u32[]{:S(2)}, u32[]{:S(2)}) %all-to-all-start.2) | async-done | bytes 262176 | tf_op jit(solution)/shard_map/all_to_all | solution.py:224
  38.1 4.7 %all-to-all-start.1 = ((bf16[8,1,128,128]{3,2,1,0:T(8,128)(2,1)}), bf16[8,1,128,128]{3,2,1,0:T(8,128)(2,1)S(1)}, u32[]{:S(2)}, u32[]{:S(2)}) async-start(bf16[8,1,128,128]{3,2,1,0:T(8,128)(2,1)} %bitcast.5), calls=%async_computation.1 | async-start | bytes 524288 | tf_op jit(solution)/shard_map/all_to_all | solution.py:223
  42.9 0.8 select_reduce_fusion.code
  43.7 8.8 %all-to-all-done.1 = bf16[8,1,128,128]{3,2,1,0:T(8,128)(2,1)S(1)} async-done(((bf16[8,1,128,128]{3,2,1,0:T(8,128)(2,1)}), bf16[8,1,128,128]{3,2,1,0:T(8,128)(2,1)S(1)}, u32[]{:S(2)}, u32[]{:S(2)}) %all-to-all-start.1) | async-done | bytes 262176 | tf_op jit(solution)/shard_map/all_to_all | solution.py:223
  52.5 0.7 copy-done.3
  53.2 43.7 %shard_map.138 = (bf16[4096,128]{1,0:T(8,128)(2,1)}, f32[4096,128]{1,0:T(8,128)}, bf16[8,128,128]{2,1,0:T(8,128)(2,1)}, f32[128,128]{1,0:T(8,128)}, f32[128,128]{1,0:T(8,128)}) custom-call(s32[32,16]{1,0:T(8,128)} %copy-done.4, s32[632]{0:T(1024)} %select_reduce_fusion.code, s32[158]{0:T(256)} %add_reduce_fusion.quad, s32[1]{0:T(128)} %bitcast.used, ...), custom_call_target="tpu_custom_call" | custom-call | tf_op jit(solution)/shard_map/pallas_call | solution.py:162
  96.9 1.7 pad_maximum_fusion
  98.6 3.4 %all-to-all-start.3 = ((bf16[8,1,128,128]{3,2,1,0:T(8,128)(2,1)}), bf16[8,1,128,128]{3,2,1,0:T(8,128)(2,1)S(1)}, u32[]{:S(2)}, u32[]{:S(2)}) async-start(bf16[8,1,128,128]{3,2,1,0:T(8,128)(2,1)} %bitcast.25), calls=%async_computation.3 | async-start | bytes 524288 | tf_op jit(solution)/shard_map/all_to_all | solution.py:240
  102.0 25.0 %reduce-scatter.2.cloned.1.call-done = f32[32,128]{1,0:T(8,128)} async-done(((f32[256,128]{1,0:T(8,128)}), f32[32,128]{1,0:T(8,128)}) %reduce-scatter.2.cloned.1.call-update) | async-done | bytes 16400 | tf_op jit(solution)/shard_map/reduce_scatter | solution.py:251
  127.0 16.5 %psum.7 = f32[32,128]{1,0:T(8,128)S(1)} all-reduce(f32[32,128]{1,0:T(8,128)} %reduce-scatter.2.cloned.1.call-done), channel_id=1, replica_groups=mesh['group'=4,'member'=8] {'group'}, use_global_device_ids=true, to_apply=%region_10.11 | all-reduce | flops 4096 | bytes 32768 | tf_op jit(solution)/shard_map/psum | solution.py:252
  143.6 13.9 %all_gather.3 = f32[256,128]{1,0:T(8,128)S(1)} all-gather(f32[32,128]{1,0:T(8,128)S(1)} %psum.7), channel_id=1, replica_groups=mesh['group'=4,'member'=8] {'member'}, dimensions={0}, use_global_device_ids=true | all-gather | bytes 147456 | tf_op jit(solution)/shard_map/all_gather | solution.py:253
  158.2 0.8 bitcast_convert_fusion
  159.0 2.0 %scatter_fusion = f32[2,128,128]{2,1,0:T(8,128)S(1)} fusion(f32[2,128,128]{2,1,0:T(8,128)S(1)} %broadcast_in_dim.99, s32[8]{0:T(128)S(1)} %fusion.2, f32[8,128,128]{2,1,0:T(8,128)} %bitcast_convert_fusion), kind=kCustom, calls=%fused_computation.3 | custom fusion | flops 131072 | bytes 1572896 | tf_op jit(solution)/shard_map/scatter-add | solution.py:247
  161.1 2.7 %scatter_fusion.1 = f32[4096,128]{1,0:T(8,128)S(1)} fusion(f32[4096,128]{1,0:T(8,128)S(1)} %copy-done.1, s32[256]{0:T(256)S(1)} %bitcast.29, f32[256,128]{1,0:T(8,128)S(1)} %bitcast.21), kind=kCustom, calls=%fused_computation.4 | custom fusion | flops 32768 | bytes 394240 | tf_op jit(solution)/shard_map/scatter-add | solution.py:248
  163.8 1.1 convert_element_type.15
  (32 shorter events, 3.3 us)
Async XLA Ops:
  7.2 16.8 %copy-start = (bf16[4096,128]{1,0:T(8,128)(2,1)S(1)}, bf16[4096,128]{1,0:T(8,128)(2,1)}, u32[]{:S(2)}) copy-start(bf16[4096,128]{1,0:T(8,128)(2,1)} %param.12) | copy-start | bytes 3145732
  8.6 19.7 %all-to-all-start = ((s32[8,1,1]{2,1,0:T(1,128)}), s32[8,1,1]{2,1,0:T(1,128)S(1)}, u32[]{:S(2)}, u32[]{:S(2)}) async-start(s32[8,1,1]{2,1,0:T(1,128)} %copy.27), calls=%async_computation | async-start | bytes 8192 | tf_op jit(solution)/shard_map/all_to_all | solution.py:221
  15.7 22.3 %copy-start.4 = (s32[32,16]{1,0:T(8,128)}, s32[32,16]{1,0:T(8,128)S(1)}, u32[]{:S(2)}) copy-start(s32[32,16]{1,0:T(8,128)S(1)} %copy.28.src) | copy-start | bytes 6148
  28.3 9.7 %all-to-all-start.2 = ((bf16[4,256,128]{2,1,0:T(8,128)(2,1)}), bf16[4,256,128]{2,1,0:T(8,128)(2,1)S(1)}, u32[]{:S(2)}, u32[]{:S(2)}) async-start(bf16[4,256,128]{2,1,0:T(8,128)(2,1)} %bitcast.7), calls=%async_computation.2 | async-start | bytes 524288 | tf_op jit(solution)/shard_map/all_to_all | solution.py:224
  38.1 14.4 %copy-start.2 = (bf16[4,256,128]{2,1,0:T(8,128)(2,1)}, bf16[4,256,128]{2,1,0:T(8,128)(2,1)S(1)}, u32[]{:S(2)}) copy-start(bf16[4,256,128]{2,1,0:T(8,128)(2,1)S(1)} %all-to-all-done.2) | copy-start | bytes 786436
  38.1 14.4 %all-to-all-start.1 = ((bf16[8,1,128,128]{3,2,1,0:T(8,128)(2,1)}), bf16[8,1,128,128]{3,2,1,0:T(8,128)(2,1)S(1)}, u32[]{:S(2)}, u32[]{:S(2)}) async-start(bf16[8,1,128,128]{3,2,1,0:T(8,128)(2,1)} %bitcast.5), calls=%async_computation.1 | async-start | bytes 524288 | tf_op jit(solution)/shard_map/all_to_all | solution.py:223
  42.8 84.3 %reduce-scatter.2.cloned.1.call-start = ((), (), s32[]{:S(2)}) async-start(), calls=%async_computation.5 | async-start | bytes 147456 | tf_op jit(solution)/shard_map/reduce_scatter | solution.py:251
  52.5 0.7 copy-start.3
  96.9 64.2 %copy-start.1 = (f32[4096,128]{1,0:T(8,128)S(1)}, f32[4096,128]{1,0:T(8,128)}, u32[]{:S(2)}) copy-start(f32[4096,128]{1,0:T(8,128)} %get-tuple-element.10) | copy-start | bytes 6291460
  98.6 59.6 %all-to-all-start.3 = ((bf16[8,1,128,128]{3,2,1,0:T(8,128)(2,1)}), bf16[8,1,128,128]{3,2,1,0:T(8,128)(2,1)S(1)}, u32[]{:S(2)}, u32[]{:S(2)}) async-start(bf16[8,1,128,128]{3,2,1,0:T(8,128)(2,1)} %bitcast.25), calls=%async_computation.3 | async-start | bytes 524288 | tf_op jit(solution)/shard_map/all_to_all | solution.py:240
Sparse Core Ops, SparseCore 0:
  98.7 28.2 reduce-scatter.1

commit v2 on v1

--- a/solution.py
+++ b/solution.py
@@ -11,6 +11,7 @@
 QUAD = 4
 F32 = jnp.float32
 BF16 = jnp.bfloat16
+MESH = pl.DeviceIdType.MESH
 
 
 def plan(tile_src, wanted_sources):
@@ -53,8 +54,7 @@
     out,
     row_grad,
     halo_grad,
-    g_self,
-    g_neigh,
+    part,
     tbuf,
     srcs,
     agg,
@@ -120,8 +120,8 @@
 
     pl.loop(0, blocks // group)(middle)
 
-    g_self[...] = gt[:, :width].T
-    g_neigh[...] = gt[:, width:].T
+    part[:width, :] = gt[:, :width].T
+    part[width:, :] = gt[:, width:].T
 
     def backward(q, acc):
         lhs, rhs = [], []
@@ -165,14 +165,13 @@
             jax.ShapeDtypeStruct((nodes, width), BF16),
             jax.ShapeDtypeStruct((nodes, width), F32),
             jax.ShapeDtypeStruct((n_halo, tile, width), BF16),
-            jax.ShapeDtypeStruct((width, width), F32),
-            jax.ShapeDtypeStruct((width, width), F32),
+            jax.ShapeDtypeStruct((2 * width, width), F32),
         ),
         in_specs=[smem] * 4
         + [vmem] * 3
         + [pl.BlockSpec(memory_space=pl.ANY)]
         + [vmem] * 4,
-        out_specs=[vmem] * 5,
+        out_specs=[vmem] * 4,
         scratch_shapes=[
             pltpu.VMEM(tiles.shape, BF16),
             pltpu.VMEM((blocks + n_halo + stale.shape[0], tile, width), BF16),
@@ -197,6 +196,303 @@
     )
 
 
+def greet(me_g, me_m, groups, members):
+    barrier = pltpu.get_barrier_semaphore()
+    for o in range(1, members):
+        pl.semaphore_signal(
+            barrier, inc=1, device_id=(me_g, lax.rem(me_m + o, members)), device_id_type=MESH
+        )
+    for o in range(1, groups):
+        pl.semaphore_signal(
+            barrier, inc=1, device_id=(lax.rem(me_g + o, groups), me_m), device_id_type=MESH
+        )
+    return lambda: pl.semaphore_wait(barrier, members + groups - 2)
+
+
+def push(src, dst, send, recv, o, device):
+    copy = pltpu.make_async_remote_copy(
+        src_ref=src,
+        dst_ref=dst,
+        send_sem=send.at[o],
+        recv_sem=recv.at[o],
+        device_id=device,
+        device_id_type=MESH,
+    )
+    copy.start()
+    return copy
+
+
+def pick_rows(row, table, depth):
+    count = row.shape[1]
+    column = jnp.broadcast_to(row, (8, count)).T[:, :1]
+    total = jnp.zeros((count, table.shape[1]), F32)
+    for c in range(0, table.shape[0], depth):
+        ids = lax.broadcasted_iota(jnp.int32, (count, depth), 1) + c
+        hot = jnp.where(ids == column, 1.0, 0.0).astype(BF16)
+        total = total + jnp.dot(hot, table[c : c + depth, :], preferred_element_type=F32)
+    return total
+
+
+def gather_kernel(
+    groups,
+    members,
+    feats,
+    hist,
+    rows,
+    picks,
+    stale_rows,
+    halo,
+    stale,
+    wanted,
+    asked,
+    bound,
+    outgoing,
+    leaving,
+    p_send,
+    p_recv,
+    h_send,
+    h_recv,
+    s_send,
+    s_recv,
+):
+    me_g, me_m = lax.axis_index("group"), lax.axis_index("member")
+    taken = picks.shape[1]
+    tile, width = halo.shape[1], halo.shape[2]
+    offered = rows.shape[1] // tile
+    each = stale_rows.shape[1] // tile
+    depth = 512
+    for p in range(members):
+        for k in range(taken):
+            asked[p, k] = jnp.broadcast_to(picks[p : p + 1, k : k + 1], asked.shape[2:])
+    entered = greet(me_g, me_m, groups, members)
+    wanted[me_m] = asked[me_m]
+    bound[...] = pick_rows(rows[...], feats, depth).reshape(offered, tile, width)
+    entered()
+    copies, calls = [], []
+    for o in range(1, members):
+        peer = lax.rem(me_m + o, members)
+        calls.append(
+            push(asked.at[peer], wanted.at[me_m], p_send, p_recv, o, (me_g, peer))
+        )
+
+    def send_stale(o):
+        to = lax.rem(me_g + o, groups)
+        found = pick_rows(stale_rows[pl.ds(to, 1), :], hist, depth)
+        found = found.astype(BF16).reshape(each, tile, width)
+        at = pl.ds(me_g * each, each)
+        if o == 0:
+            stale[at] = found
+        else:
+            leaving[o] = found
+            copies.append(push(leaving.at[o], stale.at[at], s_send, s_recv, o, (to, me_m)))
+
+    def choose(p, k):
+        w = jnp.broadcast_to(wanted[p, k][:1, :], (tile, width))
+        value = bound[0]
+        for j in range(1, offered):
+            value = jnp.where(w == j, bound[j], value)
+        return value.astype(BF16)
+
+    for o in range(groups - 1, 1, -1):
+        send_stale(o)
+    for o in range(1, members):
+        calls[o - 1].wait_recv()
+        peer = lax.rem(me_m + members - o, members)
+        for k in range(taken):
+            outgoing[o, k] = choose(peer, k)
+        at = pl.ds(me_m * taken, taken)
+        copies.append(push(outgoing.at[o], halo.at[at], h_send, h_recv, o, (me_g, peer)))
+    for k in range(taken):
+        halo[me_m * taken + k] = choose(me_m, k)
+    if groups > 1:
+        send_stale(1)
+    send_stale(0)
+    for copy in calls:
+        copy.wait_send()
+    for copy in copies:
+        copy.wait()
+
+
+def gather(features, history, boundary_rows, picks, stale_rows, tile, groups, members):
+    taken = picks.shape[1]
+    width = features.shape[1]
+    offered = boundary_rows.shape[1] // tile
+    each = stale_rows.shape[1] // tile
+    vmem = pl.BlockSpec(memory_space=pltpu.VMEM)
+    dma = pltpu.SemaphoreType.DMA
+    return pl.pallas_call(
+        functools.partial(gather_kernel, groups, members),
+        out_shape=(
+            jax.ShapeDtypeStruct((members * taken, tile, width), BF16),
+            jax.ShapeDtypeStruct((groups * each, tile, width), BF16),
+            jax.ShapeDtypeStruct((members, taken, 8, 128), jnp.int32),
+        ),
+        in_specs=[vmem] * 5,
+        out_specs=[vmem] * 3,
+        scratch_shapes=[
+            pltpu.VMEM((members, taken, 8, 128), jnp.int32),
+            pltpu.VMEM((offered, tile, width), F32),
+            pltpu.VMEM((members, taken, tile, width), BF16),
+            pltpu.VMEM((groups, each, tile, width), BF16),
+            dma((members,)),
+            dma((members,)),
+            dma((members,)),
+            dma((members,)),
+            dma((groups,)),
+            dma((groups,)),
+        ],
+        compiler_params=pltpu.CompilerParams(
+            collective_id=0, has_side_effects=True, vmem_limit_bytes=40 << 20
+        ),
+    )(features, history, boundary_rows, picks, stale_rows)
+
+
+def combine_kernel(
+    groups,
+    members,
+    factor,
+    row_grad,
+    halo_grad,
+    part,
+    wanted,
+    rows,
+    grad_features,
+    g_self,
+    g_neigh,
+    returned,
+    landed,
+    partial,
+    across,
+    share,
+    whole,
+    h_send,
+    h_recv,
+    a_send,
+    a_recv,
+    b_send,
+    b_recv,
+    c_send,
+    c_recv,
+):
+    me_g, me_m = lax.axis_index("group"), lax.axis_index("member")
+    taken = wanted.shape[1]
+    nodes, width = row_grad.shape
+    tile = halo_grad.shape[1]
+    offered = rows.shape[1] // tile
+    piece = part.shape[0] // members
+    greet(me_g, me_m, groups, members)()
+    copies, first, second, third = [], [], [], []
+    for o in range(1, members):
+        peer = lax.rem(me_m + o, members)
+        at = pl.ds(pl.multiple_of(peer * piece, piece), piece)
+        first.append(
+            push(part.at[at], landed.at[me_m], a_send, a_recv, o, (me_g, peer))
+        )
+    for o in range(1, members):
+        peer = lax.rem(me_m + o, members)
+        copies.append(
+            push(
+                halo_grad.at[pl.ds(peer * taken, taken)],
+                returned.at[me_m],
+                h_send,
+                h_recv,
+                o,
+                (me_g, peer),
+            )
+        )
+    landed[me_m] = part[pl.ds(pl.multiple_of(me_m * piece, piece), piece), :]
+    returned[me_m] = halo_grad[pl.ds(me_m * taken, taken)]
+    for copy in first:
+        copy.wait_recv()
+    total = landed[0]
+    for p in range(1, members):
+        total = total + landed[p]
+    partial[...] = total
+    across[me_g] = total
+    for o in range(1, groups):
+        to = lax.rem(me_g + o, groups)
+        second.append(push(partial, across.at[me_g], b_send, b_recv, o, (to, me_m)))
+    for copy in second:
+        copy.wait_recv()
+    total = across[0]
+    for g in range(1, groups):
+        total = total + across[g]
+    mine = pl.ds(pl.multiple_of(me_m * piece, piece), piece)
+    share[...] = total
+    whole[mine, :] = total
+    for o in range(1, members):
+        peer = lax.rem(me_m + o, members)
+        third.append(push(share, whole.at[mine], c_send, c_recv, o, (me_g, peer)))
+
+    for copy in copies:
+        copy.wait_recv()
+    halves = []
+    for j in range(offered):
+        total = jnp.zeros((tile, width), F32)
+        for p in range(members):
+            for k in range(taken):
+                w = jnp.broadcast_to(wanted[p, k][:1, :], (tile, width))
+                total = total + jnp.where(w == j, returned[p, k].astype(F32), 0.0)
+        high = total.astype(BF16)
+        low = (total - high.astype(F32)).astype(BF16)
+        halves.append(jnp.concatenate([high, low], axis=1))
+    extra = jnp.concatenate(halves, axis=0)
+    depth = 512
+
+    def add(c):
+        at = pl.ds(pl.multiple_of(c * depth, depth), depth)
+        ids = lax.broadcasted_iota(jnp.int32, (depth, rows.shape[1]), 0) + c * depth
+        hot = jnp.where(ids == rows[...], 1.0, 0.0).astype(BF16)
+        more = jnp.dot(hot, extra, preferred_element_type=F32)
+        grad_features[at, :] = (row_grad[at, :] + (more[:, :width] + more[:, width:])).astype(BF16)
+
+    pl.loop(0, nodes // depth)(add)
+    for copy in third:
+        copy.wait_recv()
+    g_self[...] = whole[:width, :] * factor
+    g_neigh[...] = whole[width:, :] * factor
+    for copy in first + second + third + copies:
+        copy.wait_send()
+
+
+def combine(row_grad, halo_grad, part, wanted, boundary_rows, groups, members, factor):
+    nodes, width = row_grad.shape
+    tile = halo_grad.shape[1]
+    taken = wanted.shape[1]
+    piece = part.shape[0] // members
+    vmem = pl.BlockSpec(memory_space=pltpu.VMEM)
+    dma = pltpu.SemaphoreType.DMA
+    return pl.pallas_call(
+        functools.partial(combine_kernel, groups, members, factor),
+        out_shape=(
+            jax.ShapeDtypeStruct((nodes, width), BF16),
+            jax.ShapeDtypeStruct((width, part.shape[1]), F32),
+            jax.ShapeDtypeStruct((width, part.shape[1]), F32),
+        ),
+        in_specs=[vmem] * 5,
+        out_specs=[vmem] * 3,
+        scratch_shapes=[
+            pltpu.VMEM((members, taken, tile, width), BF16),
+            pltpu.VMEM((members, piece, part.shape[1]), F32),
+            pltpu.VMEM((piece, part.shape[1]), F32),
+            pltpu.VMEM((groups, piece, part.shape[1]), F32),
+            pltpu.VMEM((piece, part.shape[1]), F32),
+            pltpu.VMEM(part.shape, F32),
+            dma((members,)),
+            dma((members,)),
+            dma((members,)),
+            dma((members,)),
+            dma((groups,)),
+            dma((groups,)),
+            dma((members,)),
+            dma((members,)),
+        ],
+        compiler_params=pltpu.CompilerParams(
+            collective_id=1, has_side_effects=True, vmem_limit_bytes=40 << 20
+        ),
+    )(row_grad, halo_grad, part, wanted, boundary_rows)
+
+
 def on_device(
     features,
     history,
@@ -213,46 +509,20 @@
     members = lax.axis_size("member")
     groups = lax.axis_size("group")
     tile = tiles.shape[1]
-    width = features.shape[1]
     blocks = features.shape[0] // tile
-    offered = boundary_rows.shape[1] // tile
     taken = picks.shape[1]
-    bound = features[boundary_rows[0]].reshape(offered, tile, width)
-    wanted = lax.all_to_all(picks, "member", split_axis=0, concat_axis=0, tiled=True)
-    outgoing = bound[wanted]
-    halo = lax.all_to_all(outgoing, "member", split_axis=0, concat_axis=0, tiled=True)
-    stale = lax.all_to_all(
-        history[stale_rows], "group", split_axis=0, concat_axis=0, tiled=True
-    ).reshape(-1, tile, width)
     plans = plan(tile_src, blocks + members * taken)
-    layer_out, row_grad, halo_grad, part_self, part_neigh = local(
-        tile_src,
-        plans,
-        features,
-        halo.reshape(-1, tile, width),
-        stale,
-        tiles,
-        degree,
-        w_self,
-        w_neigh,
-        cotangent,
-    )
-    returned = lax.all_to_all(
-        halo_grad.reshape(members, taken, tile, width),
-        "member",
-        split_axis=0,
-        concat_axis=0,
-        tiled=True,
-    ).astype(F32)
-    bound_grad = jnp.zeros((offered, tile, width), F32).at[wanted].add(returned)
-    row_grad = row_grad.at[boundary_rows[0]].add(bound_grad.reshape(-1, width))
-    grad_features = row_grad.astype(BF16)
-    parts = jnp.concatenate([part_self, part_neigh], axis=0)
-    share = lax.psum_scatter(parts, "member", scatter_dimension=0, tiled=True)
-    share = lax.psum(share, "group")
-    whole = lax.all_gather(share, "member", axis=0, tiled=True)
+    halo, stale, wanted = gather(
+        features, history, boundary_rows, picks, stale_rows, tile, groups, members
+    )
+    layer_out, row_grad, halo_grad, part = local(
+        tile_src, plans, features, halo, stale, tiles, degree, w_self, w_neigh, cotangent
+    )
     factor = 1.0 / math.sqrt(features.shape[0] * members * groups)
-    return (layer_out, grad_features, whole[:width] * factor, whole[width:] * factor)
+    grad_features, grad_self, grad_neigh = combine(
+        row_grad, halo_grad, part, wanted, boundary_rows, groups, members, factor
+    )
+    return (layer_out, grad_features, grad_self, grad_neigh)
 
 
 def solution(mesh):

time: 173 us -> 93.9 us (0.54)
  waiting for transfers between devices: 38.3 us -> 0 us
  Pallas kernels: 43.7 us -> 74.8 us
  blocking collectives: 30.5 us -> 0 us
  starting transfers between devices: 18.2 us -> 0 us
  between operations: 16.7 us -> 3.31 us
  other arithmetic: 13.4 us -> 2.75 us
  local copies, waits for them, and re-layouts: 10.9 us -> 12.7 us
    pallas_call x0 -> x2, Pallas kernels: none -> 32.3 us  [the longest x1 16.9 us: combine(): pl.pallas_call(functools.partial(combine_kernel, groups, members, factor)...]
    reduce_scatter x1 -> x0, waiting for transfers between devices: 25 us -> none  [on_device(): share = lax.psum_scatter(parts, 'member', scatter_dimension=0, tiled=True)]
    all_to_all x4 -> x0, starting transfers between devices: 18.2 us -> none  [the longest x1 6.35 us: on_device(): lax.all_to_all(picks, 'member', split_axis=0, concat_axis=0, tiled=True)]
    psum x1 -> x0, blocking collectives: 16.5 us -> none  [on_device(): share = lax.psum(share, 'group')]
    all_gather x1 -> x0, blocking collectives: 13.9 us -> none  [on_device(): whole = lax.all_gather(share, 'member', axis=0, tiled=True)]
    all_to_all x4 -> x0, waiting for transfers between devices: 13.3 us -> none  [the longest x1 8.76 us: on_device(): lax.all_to_all(outgoing, 'member', split_axis=0, concat_axis=0, tiled=True)]
    unnamed x12 -> x27, local copies, waits for them, and re-layouts: 1.5 us -> 12.4 us
    gather x3 -> x0, local copies, waits for them, and re-layouts: 7.68 us -> none  [the longest x1 4.31 us: on_device(): history[stale_rows]]
  transfers between devices with their start and end apart: 5 -> 0, of which waited for: 3 -> 0; matrix products, arithmetic and copies ran while one was open for 8% -> 0% of each run, Pallas kernels for 0% -> 0%
where the time goes in v2:
time: 93.9 us; the launch traced here: 93.6 us
  Pallas kernels  74.8 us (80%)
  local copies, waits for them, and re-layouts  12.7 us (14%)
  between operations  3.31 us (4%)
  other arithmetic  2.75 us (3%)
    pallas_call x1, Pallas kernels, local(): pl.pallas_call(local_kernel, out_shape=(jax.ShapeDtypeStruct((nodes, widt...  42.5 us
    pallas_call x1, Pallas kernels, combine(): pl.pallas_call(functools.partial(combine_kernel, groups, members, factor)...  16.9 us
    pallas_call x1, Pallas kernels, gather(): pl.pallas_call(functools.partial(gather_kernel, groups, members), out_sha...  15.4 us
    unnamed x27, local copies, waits for them, and re-layouts  12.4 us

profile of v2, /device:TPU:0, one launch (start us, length us, event | category | flops | bytes accessed | tf_op | source)
XLA Modules:
  0.0 93.6 jit_solution(9193792831678318677)
XLA Ops:
  0.6 0.7 copy.21.picks
  1.4 0.2 slice.7
  1.6 0.8 copy.22.src
  2.5 0.1 convert_reduce_fusion
  2.6 0.7 fusion.2
  5.8 0.1 select_reduce_fusion.3
  5.9 0.7 add_reduce_fusion.quad
  6.7 0.3 select_reduce_fusion.1
  7.0 0.8 select_reduce_fusion.code
  7.8 1.2 %copy-done = bf16[4096,128]{1,0:T(8,128)(2,1)S(1)} copy-done((bf16[4096,128]{1,0:T(8,128)(2,1)S(1)}, bf16[4096,128]{1,0:T(8,128)(2,1)}, u32[]{:S(2)}) %copy-start) | copy-done | bytes 1048600
  9.0 1.2 %copy-done.2 = bf16[4096,128]{1,0:T(8,128)(2,1)S(1)} copy-done((bf16[4096,128]{1,0:T(8,128)(2,1)S(1)}, bf16[4096,128]{1,0:T(8,128)(2,1)}, u32[]{:S(2)}) %copy-start.2) | copy-done | bytes 1048600
  10.3 0.7 copy-done.7
  11.0 0.7 copy-done.8
  11.6 15.4 %shard_map.138 = (bf16[8,128,128]{2,1,0:T(8,128)(2,1)S(1)}, bf16[8,128,128]{2,1,0:T(8,128)(2,1)S(1)}, s32[8,1,8,128]{3,2,1,0:T(8,128)S(1)}) custom-call(bf16[4096,128]{1,0:T(8,128)(2,1)S(1)} %copy-done, bf16[4096,128]{1,0:T(8,128)(2,1)S(1)} %copy-done.2, s32[1,256]{1,0:T(1,128)S(1)} %copy-done.8, s32[8,1]{1,0:T(8,128)S(1)} %copy.21.picks, s32[4,256]{1,0:T(4,128)S(1)} %copy-done.7), custom_call_target="tpu_custom_call" | custom-call | tf_op jit(solution)/shard_map/pallas_call | solution.py:323
  27.1 0.7 copy-done.3
  27.8 0.7 copy-done.4
  28.5 42.5 %shard_map.139 = (bf16[4096,128]{1,0:T(8,128)(2,1)}, f32[4096,128]{1,0:T(8,128)}, bf16[8,128,128]{2,1,0:T(8,128)(2,1)}, f32[256,128]{1,0:T(8,128)}) custom-call(s32[32,16]{1,0:T(8,128)} %copy-done.10, s32[632]{0:T(1024)} %select_reduce_fusion.code, s32[158]{0:T(256)} %add_reduce_fusion.quad, s32[1]{0:T(128)} %bitcast.used, bf16[4096,128]{1,0:T(8,128)(2,1)} %feats.3, ...), custom_call_target="tpu_custom_call" | custom-call | tf_op jit(solution)/shard_map/pallas_call | solution.py:162
  71.0 1.6 %copy-done.1 = f32[4096,128]{1,0:T(8,128)S(1)} copy-done((f32[4096,128]{1,0:T(8,128)S(1)}, f32[4096,128]{1,0:T(8,128)}, u32[]{:S(2)}) %copy-start.1) | copy-done | bytes 2097176
  72.6 0.9 %copy-done.5 = bf16[8,128,128]{2,1,0:T(8,128)(2,1)S(1)} copy-done((bf16[8,128,128]{2,1,0:T(8,128)(2,1)S(1)}, bf16[8,128,128]{2,1,0:T(8,128)(2,1)}, u32[]{:S(2)}) %copy-start.5) | copy-done | bytes 262168
  73.5 0.9 copy-done.6
  74.4 16.9 %shard_map.140 = (bf16[4096,128]{1,0:T(8,128)(2,1)S(1)}, f32[128,128]{1,0:T(8,128)S(1)}, f32[128,128]{1,0:T(8,128)S(1)}) custom-call(f32[4096,128]{1,0:T(8,128)S(1)} %copy-done.1, bf16[8,128,128]{2,1,0:T(8,128)(2,1)S(1)} %copy-done.5, f32[256,128]{1,0:T(8,128)S(1)} %copy-done.6, s32[8,1,8,128]{3,2,1,0:T(8,128)S(1)} %get-tuple-element.20.wanted, ...), custom_call_target="tpu_custom_call" | custom-call | tf_op jit(solution)/shard_map/pallas_call | solution.py:465
  91.3 1.0 %copy.26 = bf16[4096,128]{1,0:T(8,128)(2,1)} copy(bf16[4096,128]{1,0:T(8,128)(2,1)S(1)} %get-tuple-element.33) | data formatting | bytes 2097152
  92.3 0.6 copy.27
  93.0 0.6 copy.28
  (19 shorter events, 0.2 us)
Async XLA Ops:
  2.4 26.1 %copy-start.10 = (s32[32,16]{1,0:T(8,128)}, s32[32,16]{1,0:T(8,128)S(1)}, u32[]{:S(2)}) copy-start(s32[32,16]{1,0:T(8,128)S(1)} %copy.22.src) | copy-start | bytes 6148
  7.8 1.2 %copy-start = (bf16[4096,128]{1,0:T(8,128)(2,1)S(1)}, bf16[4096,128]{1,0:T(8,128)(2,1)}, u32[]{:S(2)}) copy-start(bf16[4096,128]{1,0:T(8,128)(2,1)} %feats.3) | copy-start | bytes 3145732
  9.0 1.2 %copy-start.2 = (bf16[4096,128]{1,0:T(8,128)(2,1)S(1)}, bf16[4096,128]{1,0:T(8,128)(2,1)}, u32[]{:S(2)}) copy-start(bf16[4096,128]{1,0:T(8,128)(2,1)} %hist.1) | copy-start | bytes 3145732
  10.3 0.7 copy-start.7
  11.0 0.7 copy-start.8
  27.0 0.7 copy-start.3
  27.8 0.7 copy-start.4
  28.5 42.5 %copy-start.9 = (s32[1,256]{1,0:T(1,128)S(1)}, s32[1,256]{1,0:T(1,128)}, u32[]{:S(2)}) copy-start(s32[1,256]{1,0:T(1,128)} %rows.3) | copy-start | bytes 3076
  71.0 1.6 %copy-start.1 = (f32[4096,128]{1,0:T(8,128)S(1)}, f32[4096,128]{1,0:T(8,128)}, u32[]{:S(2)}) copy-start(f32[4096,128]{1,0:T(8,128)} %get-tuple-element.17.row_grad) | copy-start | bytes 6291460
  72.6 0.9 %copy-start.5 = (bf16[8,128,128]{2,1,0:T(8,128)(2,1)S(1)}, bf16[8,128,128]{2,1,0:T(8,128)(2,1)}, u32[]{:S(2)}) copy-start(bf16[8,128,128]{2,1,0:T(8,128)(2,1)} %get-tuple-element.18.halo_grad) | copy-start | bytes 786436
  73.5 0.9 copy-start.6

commit v3 on v2

--- a/solution.py
+++ b/solution.py
@@ -9,6 +9,7 @@
 from jax.sharding import PartitionSpec as P
 
 QUAD = 4
+STEP = 8
 F32 = jnp.float32
 BF16 = jnp.bfloat16
 MESH = pl.DeviceIdType.MESH
@@ -18,6 +19,7 @@
     flat = tile_src.reshape(-1)
     total = flat.shape[0]
     slots = (total + wanted_sources * (QUAD - 1)) // QUAD * QUAD
+    slots = -(-slots // (QUAD * STEP)) * QUAD * STEP
     index = jnp.arange(total, dtype=jnp.int32)
     same = flat[:, None] == flat[None, :]
     within = jnp.sum(jnp.where(same & (index[None, :] < index[:, None]), 1, 0), axis=1)
@@ -34,7 +36,9 @@
     inside = (offset[None, :] <= first[:, None]) & (first[:, None] < (offset + padded)[None, :])
     start = inside & (offset[None, :] == first[:, None])
     quad = jnp.sum(jnp.where(inside, 2 * ids[None, :], 0) + start.astype(jnp.int32), axis=1)
-    used = (jnp.sum(padded) // QUAD).reshape(1)
+    end = jnp.sum(padded)
+    quad = jnp.where(first < end, quad, 2 * wanted_sources + 1)
+    used = ((end // QUAD + STEP - 1) // STEP).reshape(1)
     return code, quad, used
 
 
@@ -94,7 +98,7 @@
     pl.loop(0, blocks, unroll=2)(forward)
 
     gt[...] = jnp.zeros_like(gt)
-    group = 4
+    group = 8
     rows = group * tile
     w_cat = jnp.concatenate([w_self[...], w_neigh[...]], axis=0)
 
@@ -123,22 +127,27 @@
     part[:width, :] = gt[:, :width].T
     part[width:, :] = gt[:, width:].T
 
-    def backward(q, acc):
-        lhs, rhs = [], []
-        for i in range(QUAD):
-            k = code[q * QUAD + i]
-            t = jnp.maximum(k - 1, 0)
-            b = jnp.where(k == 0, blocks, t // per)
-            lhs.append(back[b])
-            rhs.append(tbuf[t])
-        term = jnp.dot(
-            jnp.concatenate(lhs, axis=1),
-            jnp.concatenate(rhs, axis=0),
-            preferred_element_type=F32,
-        )
-        info = quad[q]
-        acc = term + jnp.where(info % 2 == 1, 0.0, acc)
-        grad[info // 2] = acc
+    def backward(step, acc):
+        terms = []
+        for u in range(STEP):
+            lhs, rhs = [], []
+            for i in range(QUAD):
+                k = code[(step * STEP + u) * QUAD + i]
+                t = jnp.maximum(k - 1, 0)
+                b = jnp.where(k == 0, blocks, t // per)
+                lhs.append(back[b])
+                rhs.append(tbuf[t])
+            terms.append(
+                jnp.dot(
+                    jnp.concatenate(lhs, axis=1),
+                    jnp.concatenate(rhs, axis=0),
+                    preferred_element_type=F32,
+                )
+            )
+        for u in range(STEP):
+            info = quad[step * STEP + u]
+            acc = terms[u] + jnp.where(info % 2 == 1, 0.0, acc)
+            grad[info // 2] = acc
         return acc
 
     lax.fori_loop(0, used[0], backward, jnp.zeros((width, tile), F32))
@@ -177,7 +186,7 @@
             pltpu.VMEM((blocks + n_halo + stale.shape[0], tile, width), BF16),
             pltpu.VMEM((nodes, width), BF16),
             pltpu.VMEM((blocks + 1, width, tile), BF16),
-            pltpu.VMEM((blocks + n_halo, width, tile), F32),
+            pltpu.VMEM((blocks + n_halo + 1, width, tile), F32),
             pltpu.VMEM((width, 2 * width), F32),
             pltpu.SemaphoreType.DMA((blocks,)),
         ],
@@ -236,8 +245,8 @@
 def gather_kernel(
     groups,
     members,
-    feats,
-    hist,
+    feats_in,
+    hist_in,
     rows,
     picks,
     stale_rows,
@@ -245,9 +254,12 @@
     stale,
     wanted,
     asked,
+    feats,
+    hist,
     bound,
     outgoing,
     leaving,
+    l_sems,
     p_send,
     p_recv,
     h_send,
@@ -261,13 +273,19 @@
     offered = rows.shape[1] // tile
     each = stale_rows.shape[1] // tile
     depth = 512
+    load_feats = pltpu.make_async_copy(feats_in, feats, l_sems.at[0])
+    load_hist = pltpu.make_async_copy(hist_in, hist, l_sems.at[1])
+    load_feats.start()
+    load_hist.start()
     for p in range(members):
         for k in range(taken):
             asked[p, k] = jnp.broadcast_to(picks[p : p + 1, k : k + 1], asked.shape[2:])
     entered = greet(me_g, me_m, groups, members)
     wanted[me_m] = asked[me_m]
+    load_feats.wait()
     bound[...] = pick_rows(rows[...], feats, depth).reshape(offered, tile, width)
     entered()
+    load_hist.wait()
     copies, calls = [], []
     for o in range(1, members):
         peer = lax.rem(me_m + o, members)
@@ -327,13 +345,16 @@
             jax.ShapeDtypeStruct((groups * each, tile, width), BF16),
             jax.ShapeDtypeStruct((members, taken, 8, 128), jnp.int32),
         ),
-        in_specs=[vmem] * 5,
+        in_specs=[pl.BlockSpec(memory_space=pl.ANY)] * 2 + [vmem] * 3,
         out_specs=[vmem] * 3,
         scratch_shapes=[
             pltpu.VMEM((members, taken, 8, 128), jnp.int32),
+            pltpu.VMEM(features.shape, BF16),
+            pltpu.VMEM(history.shape, BF16),
             pltpu.VMEM((offered, tile, width), F32),
             pltpu.VMEM((members, taken, tile, width), BF16),
             pltpu.VMEM((groups, each, tile, width), BF16),
+            dma((2,)),
             dma((members,)),
             dma((members,)),
             dma((members,)),
@@ -342,7 +363,7 @@
             dma((groups,)),
         ],
         compiler_params=pltpu.CompilerParams(
-            collective_id=0, has_side_effects=True, vmem_limit_bytes=40 << 20
+            collective_id=0, has_side_effects=True, vmem_limit_bytes=60 << 20
         ),
     )(features, history, boundary_rows, picks, stale_rows)
 
@@ -351,7 +372,7 @@
     groups,
     members,
     factor,
-    row_grad,
+    row_grad_in,
     halo_grad,
     part,
     wanted,
@@ -359,6 +380,8 @@
     grad_features,
     g_self,
     g_neigh,
+    row_grad,
+    l_sem,
     returned,
     landed,
     partial,
@@ -380,6 +403,8 @@
     tile = halo_grad.shape[1]
     offered = rows.shape[1] // tile
     piece = part.shape[0] // members
+    load = pltpu.make_async_copy(row_grad_in, row_grad, l_sem)
+    load.start()
     greet(me_g, me_m, groups, members)()
     copies, first, second, third = [], [], [], []
     for o in range(1, members):
@@ -437,6 +462,7 @@
         low = (total - high.astype(F32)).astype(BF16)
         halves.append(jnp.concatenate([high, low], axis=1))
     extra = jnp.concatenate(halves, axis=0)
+    load.wait()
     depth = 512
 
     def add(c):
@@ -469,9 +495,11 @@
             jax.ShapeDtypeStruct((width, part.shape[1]), F32),
             jax.ShapeDtypeStruct((width, part.shape[1]), F32),
         ),
-        in_specs=[vmem] * 5,
+        in_specs=[pl.BlockSpec(memory_space=pl.ANY)] + [vmem] * 4,
         out_specs=[vmem] * 3,
         scratch_shapes=[
+            pltpu.VMEM((nodes, width), F32),
+            dma(()),
             pltpu.VMEM((members, taken, tile, width), BF16),
             pltpu.VMEM((members, piece, part.shape[1]), F32),
             pltpu.VMEM((piece, part.shape[1]), F32),
@@ -488,7 +516,7 @@
             dma((members,)),
         ],
         compiler_params=pltpu.CompilerParams(
-            collective_id=1, has_side_effects=True, vmem_limit_bytes=40 << 20
+            collective_id=1, has_side_effects=True, vmem_limit_bytes=60 << 20
         ),
     )(row_grad, halo_grad, part, wanted, boundary_rows)
 

time: 93.9 us -> 75.1 us (0.80)
  Pallas kernels: 74.8 us -> 62.2 us
  local copies, waits for them, and re-layouts: 12.7 us -> 5.96 us
    pallas_call x1, Pallas kernels: 42.5 us -> 26.6 us  [local(): pl.pallas_call(local_kernel, out_shape=(jax.ShapeDtypeStruct((nodes, widt...]
    unnamed x27 -> x11, local copies, waits for them, and re-layouts: 12.4 us -> 5.67 us
    pallas_call x1, Pallas kernels: 16.9 us -> 18.6 us  [combine(): pl.pallas_call(functools.partial(combine_kernel, groups, members, factor)...]
    pallas_call x1, Pallas kernels: 15.4 us -> 17 us  [gather(): pl.pallas_call(functools.partial(gather_kernel, groups, members), out_sha...]
    select_n x0 -> x1, other arithmetic: none -> 1.18 us  [plan(): quad = jnp.where(first < end, quad, 2 * wanted_sources + 1)]
where the time goes in v3:
time: 75.1 us; the launch traced here: 74.8 us
  Pallas kernels  62.2 us (83%)
  local copies, waits for them, and re-layouts  5.96 us (8%)
  other arithmetic  3.36 us (4%)
  between operations  3.33 us (4%)
    pallas_call x1, Pallas kernels, local(): pl.pallas_call(local_kernel, out_shape=(jax.ShapeDtypeStruct((nodes, widt...  26.6 us
    pallas_call x1, Pallas kernels, combine(): pl.pallas_call(functools.partial(combine_kernel, groups, members, factor)...  18.6 us
    pallas_call x1, Pallas kernels, gather(): pl.pallas_call(functools.partial(gather_kernel, groups, members), out_sha...  17 us
    unnamed x11, local copies, waits for them, and re-layouts  5.67 us

profile of v3, /device:TPU:0, one launch (start us, length us, event | category | flops | bytes accessed | tf_op | source)
XLA Modules:
  0.0 74.8 jit_solution(8077178479309528090)
XLA Ops:
  0.6 1.3 %copy.21.picks = s32[8,1]{1,0:T(8,128)} copy(s32[8,1]{0,1:T(1,128)} %param.17) | data formatting | bytes 64 | tf_op args[6]
  2.0 0.2 slice.9
  2.2 0.8 %copy.22.src = s32[32,16]{1,0:T(8,128)S(1)} copy(s32[32,16]{0,1:T(8,128)} %param.14) | data formatting | bytes 4096 | tf_op args[3]
  3.0 0.0 copy-start
  3.0 0.1 reshape.67
  3.0 0.1 convert_reduce_fusion
  3.2 0.7 fusion.2
  6.4 0.1 select_reduce_fusion.3
  6.6 0.1 add_reduce_fusion
  6.7 1.2 %compare_select_fusion.quad = s32[160]{0:T(256)} fusion(s32[160]{0:T(256)S(1)} %add_reduce_fusion, s32[160]{0:T(256)S(1)} %slice.9, s32[]{:T(128)} %get-tuple-element.24), kind=kLoop, calls=%fused_computation.13 | loop fusion | flops 320 | bytes 1924 | tf_op jit(solution)/shard_map/jit(_where)/select_n | solution.py:40
  7.8 0.1 select_reduce_fusion.2
  7.9 0.3 select_reduce_fusion.1
  8.2 0.8 %select_reduce_fusion.code = s32[640]{0:T(1024)} fusion(s32[512]{0:T(512)S(1)} %get-tuple-element.26, s32[512]{0:T(512)S(1)} %get-tuple-element.27), kind=kLoop, calls=%fused_computation | loop fusion | flops 982400 | bytes 6656 | tf_op jit(solution)/shard_map/reduce_sum | solution.py:34
  9.0 17.0 %shard_map.138 = (bf16[8,128,128]{2,1,0:T(8,128)(2,1)}, bf16[8,128,128]{2,1,0:T(8,128)(2,1)}, s32[8,1,8,128]{3,2,1,0:T(8,128)}) custom-call(bf16[4096,128]{1,0:T(8,128)(2,1)} %feats.1, bf16[4096,128]{1,0:T(8,128)(2,1)} %hist_in.1, s32[1,256]{1,0:T(1,128)} %rows.3, s32[8,1]{1,0:T(8,128)} %copy.21.picks, s32[4,256]{1,0:T(4,128)} %stale_rows.1), custom_call_target="tpu_custom_call" | custom-call | tf_op jit(solution)/shard_map/pallas_call | solution.py:341
  26.0 0.0 copy-done
  26.0 26.6 %shard_map.139 = (bf16[4096,128]{1,0:T(8,128)(2,1)}, f32[4096,128]{1,0:T(8,128)}, bf16[8,128,128]{2,1,0:T(8,128)(2,1)}, f32[256,128]{1,0:T(8,128)}) custom-call(s32[32,16]{1,0:T(8,128)} %copy-done, s32[640]{0:T(1024)} %select_reduce_fusion.code, s32[160]{0:T(256)} %compare_select_fusion.quad, s32[1]{0:T(128)} %bitcast.used, bf16[4096,128]{1,0:T(8,128)(2,1)} %feats.1, ...), custom_call_target="tpu_custom_call" | custom-call | tf_op jit(solution)/shard_map/pallas_call | solution.py:171
  52.6 18.6 %shard_map.140 = (bf16[4096,128]{1,0:T(8,128)(2,1)}, f32[128,128]{1,0:T(8,128)}, f32[128,128]{1,0:T(8,128)}) custom-call(f32[4096,128]{1,0:T(8,128)} %get-tuple-element.17.row_grad_in, bf16[8,128,128]{2,1,0:T(8,128)(2,1)} %get-tuple-element.18.halo_grad, f32[256,128]{1,0:T(8,128)} %get-tuple-element.19.part, s32[8,1,8,128]{3,2,1,0:T(8,128)} %get-tuple-element.20.wanted, ...), custom_call_target="tpu_custom_call" | custom-call | tf_op jit(solution)/shard_map/pallas_call | solution.py:491
  71.2 0.0 copy-start.2
  71.2 0.0 copy-start.1
  71.3 2.3 %copy.26 = bf16[4096,128]{1,0:T(8,128)(2,1)} copy(bf16[4096,128]{1,0:T(8,128)(2,1)} %get-tuple-element.33) | data formatting | bytes 2097152
  73.5 0.0 copy-done.2
  73.6 0.6 copy.27
  74.2 0.0 copy-done.1
  74.2 0.6 copy.28
  (4 shorter events, 0.0 us)
Async XLA Ops:
  3.0 23.0 %copy-start = (s32[32,16]{1,0:T(8,128)}, s32[32,16]{1,0:T(8,128)S(1)}, u32[]{:S(2)}) copy-start(s32[32,16]{1,0:T(8,128)S(1)} %copy.22.src) | copy-start | bytes 6148
  71.2 2.3 %copy-start.2 = (f32[128,128]{1,0:T(8,128)S(1)}, f32[128,128]{1,0:T(8,128)}, u32[]{:S(2)}) copy-start(f32[128,128]{1,0:T(8,128)} %get-tuple-element.34) | copy-start | bytes 196612
  71.2 2.9 %copy-start.1 = (f32[128,128]{1,0:T(8,128)S(1)}, f32[128,128]{1,0:T(8,128)}, u32[]{:S(2)}) copy-start(f32[128,128]{1,0:T(8,128)} %get-tuple-element.35) | copy-start | bytes 196612

commit v4 on v3

--- a/solution.py
+++ b/solution.py
@@ -15,31 +15,45 @@
 MESH = pl.DeviceIdType.MESH
 
 
-def plan(tile_src, wanted_sources):
-    flat = tile_src.reshape(-1)
-    total = flat.shape[0]
-    slots = (total + wanted_sources * (QUAD - 1)) // QUAD * QUAD
-    slots = -(-slots // (QUAD * STEP)) * QUAD * STEP
-    index = jnp.arange(total, dtype=jnp.int32)
-    same = flat[:, None] == flat[None, :]
-    within = jnp.sum(jnp.where(same & (index[None, :] < index[:, None]), 1, 0), axis=1)
-    ids = jnp.arange(wanted_sources, dtype=jnp.int32)
-    hit = flat[None, :] == ids[:, None]
-    count = jnp.sum(hit.astype(jnp.int32), axis=1)
-    padded = (count + QUAD - 1) // QUAD * QUAD
-    offset = jnp.sum(jnp.where(ids[None, :] < ids[:, None], padded[None, :], 0), axis=1)
-    base = jnp.sum(jnp.where(hit, offset[:, None], 0), axis=0)
-    pos = jnp.where(flat < wanted_sources, base + within, -1)
-    slot = jnp.arange(slots, dtype=jnp.int32)
-    code = jnp.sum(jnp.where(pos[None, :] == slot[:, None], index[None, :] + 1, 0), axis=1)
-    first = slot[::QUAD]
-    inside = (offset[None, :] <= first[:, None]) & (first[:, None] < (offset + padded)[None, :])
-    start = inside & (offset[None, :] == first[:, None])
-    quad = jnp.sum(jnp.where(inside, 2 * ids[None, :], 0) + start.astype(jnp.int32), axis=1)
-    end = jnp.sum(padded)
-    quad = jnp.where(first < end, quad, 2 * wanted_sources + 1)
-    used = ((end // QUAD + STEP - 1) // STEP).reshape(1)
-    return code, quad, used
+def plan_sizes(total, wanted_sources):
+    slots = total + wanted_sources * (QUAD - 1)
+    slots = -(-slots // 128) * 128
+    return slots, -(-(slots // QUAD) // 128) * 128
+
+
+def plan(row, wanted_sources, slots, quads):
+    total = row.shape[1]
+    wide = -(-wanted_sources // 128) * 128
+
+    def iota(shape, axis):
+        return lax.broadcasted_iota(jnp.int32, shape, axis).astype(F32)
+
+    def column(value):
+        return jnp.broadcast_to(value, (8, value.shape[1])).T[:, :1]
+
+    row = row.astype(F32)
+    square = (total, total)
+    same = (column(row) == row) & (iota(square, 0) < iota(square, 1))
+    within = jnp.sum(jnp.where(same, 1.0, 0.0), axis=0, keepdims=True)
+    ids = iota((wide, total), 0)
+    hit = (ids == row) & (ids < wanted_sources)
+    count = jnp.sum(jnp.where(hit, 1.0, 0.0), axis=1, keepdims=True)
+    need = jnp.floor((count + (QUAD - 1)) / QUAD)
+    spread = jnp.broadcast_to(need, (wide, wide)).T
+    before = iota((wide, wide), 1) < iota((wide, wide), 0)
+    offset = jnp.sum(jnp.where(before, spread, 0.0), axis=1, keepdims=True)
+    end = jnp.sum(spread[:1, :], axis=1, keepdims=True)
+    base = jnp.sum(jnp.where(hit, QUAD * offset, 0.0), axis=0, keepdims=True)
+    pos = jnp.where(row < wanted_sources, base + within, -1.0)
+    here = column(pos) == iota((total, slots), 1)
+    code = jnp.sum(jnp.where(here, iota((total, slots), 0) + 1.0, 0.0), axis=0, keepdims=True)
+    q = iota((wide, quads), 1)
+    inside = (offset <= q) & (q < offset + need)
+    info = 2.0 * iota((wide, quads), 0) + jnp.where(offset == q, 1.0, 0.0)
+    quad = jnp.sum(jnp.where(inside, info, 0.0), axis=0, keepdims=True)
+    quad = jnp.where(q[:1, :] < end, quad, 2.0 * wanted_sources + 1.0)
+    used = jnp.broadcast_to(jnp.floor((end + (STEP - 1)) / STEP), (1, 128))
+    return code.astype(jnp.int32), quad.astype(jnp.int32), used.astype(jnp.int32)
 
 
 def local_kernel(
@@ -67,7 +81,8 @@
     gt,
     sems,
 ):
-    blocks, per = src.shape
+    blocks = deg.shape[0]
+    per = src.shape[1] // blocks
     tile, width = feats.shape[0] // blocks, feats.shape[1]
     n_halo, n_stale = halo.shape[0], stale.shape[0]
 
@@ -90,7 +105,7 @@
     def forward(b):
         chunk(b).wait()
         lhs = jnp.concatenate([tbuf[b * per + t] for t in range(per)], axis=1)
-        rhs = jnp.concatenate([srcs[src[b, t]] for t in range(per)], axis=0)
+        rhs = jnp.concatenate([srcs[src[0, b * per + t]] for t in range(per)], axis=0)
         total = jnp.dot(lhs, rhs, preferred_element_type=F32)
         d = jnp.broadcast_to(deg[pl.ds(b, 1), :].astype(F32), (tile, tile)).T
         agg[pl.ds(pl.multiple_of(b * tile, tile), tile), :] = (total / d).astype(BF16)
@@ -132,7 +147,7 @@
         for u in range(STEP):
             lhs, rhs = [], []
             for i in range(QUAD):
-                k = code[(step * STEP + u) * QUAD + i]
+                k = code[0, (step * STEP + u) * QUAD + i]
                 t = jnp.maximum(k - 1, 0)
                 b = jnp.where(k == 0, blocks, t // per)
                 lhs.append(back[b])
@@ -145,12 +160,12 @@
                 )
             )
         for u in range(STEP):
-            info = quad[step * STEP + u]
+            info = quad[0, step * STEP + u]
             acc = terms[u] + jnp.where(info % 2 == 1, 0.0, acc)
             grad[info // 2] = acc
         return acc
 
-    lax.fori_loop(0, used[0], backward, jnp.zeros((width, tile), F32))
+    lax.fori_loop(0, used[0, 0], backward, jnp.zeros((width, tile), F32))
 
     def finish(b):
         at = pl.ds(pl.multiple_of(b * tile, tile), tile)
@@ -162,9 +177,9 @@
 
 
 def local(tile_src, plans, features, halo, stale, tiles, degree, w_self, w_neigh, cotangent):
-    blocks, per = tile_src.shape
     tile = tiles.shape[1]
     nodes, width = features.shape
+    blocks = nodes // tile
     n_halo = halo.shape[0]
     smem = pl.BlockSpec(memory_space=pltpu.SMEM)
     vmem = pl.BlockSpec(memory_space=pltpu.VMEM)
@@ -250,9 +265,13 @@
     rows,
     picks,
     stale_rows,
+    tile_src,
     halo,
     stale,
     wanted,
+    code,
+    quad,
+    used,
     asked,
     feats,
     hist,
@@ -325,17 +344,23 @@
     if groups > 1:
         send_stale(1)
     send_stale(0)
+    blocks = feats.shape[0] // tile
+    code[...], quad[...], used[...] = plan(
+        tile_src[...], blocks + members * taken, code.shape[1], quad.shape[1]
+    )
     for copy in calls:
         copy.wait_send()
     for copy in copies:
         copy.wait()
 
 
-def gather(features, history, boundary_rows, picks, stale_rows, tile, groups, members):
+def gather(features, history, boundary_rows, picks, stale_rows, tile_src, tile, groups, members):
     taken = picks.shape[1]
     width = features.shape[1]
     offered = boundary_rows.shape[1] // tile
     each = stale_rows.shape[1] // tile
+    wanted_sources = features.shape[0] // tile + members * taken
+    slots, quads = plan_sizes(tile_src.shape[1], wanted_sources)
     vmem = pl.BlockSpec(memory_space=pltpu.VMEM)
     dma = pltpu.SemaphoreType.DMA
     return pl.pallas_call(
@@ -344,9 +369,12 @@
             jax.ShapeDtypeStruct((members * taken, tile, width), BF16),
             jax.ShapeDtypeStruct((groups * each, tile, width), BF16),
             jax.ShapeDtypeStruct((members, taken, 8, 128), jnp.int32),
+            jax.ShapeDtypeStruct((1, slots), jnp.int32),
+            jax.ShapeDtypeStruct((1, quads), jnp.int32),
+            jax.ShapeDtypeStruct((1, 128), jnp.int32),
         ),
-        in_specs=[pl.BlockSpec(memory_space=pl.ANY)] * 2 + [vmem] * 3,
-        out_specs=[vmem] * 3,
+        in_specs=[pl.BlockSpec(memory_space=pl.ANY)] * 2 + [vmem] * 4,
+        out_specs=[vmem] * 6,
         scratch_shapes=[
             pltpu.VMEM((members, taken, 8, 128), jnp.int32),
             pltpu.VMEM(features.shape, BF16),
@@ -365,7 +393,7 @@
         compiler_params=pltpu.CompilerParams(
             collective_id=0, has_side_effects=True, vmem_limit_bytes=60 << 20
         ),
-    )(features, history, boundary_rows, picks, stale_rows)
+    )(features, history, boundary_rows, picks, stale_rows, tile_src)
 
 
 def combine_kernel(
@@ -537,11 +565,9 @@
     members = lax.axis_size("member")
     groups = lax.axis_size("group")
     tile = tiles.shape[1]
-    blocks = features.shape[0] // tile
-    taken = picks.shape[1]
-    plans = plan(tile_src, blocks + members * taken)
-    halo, stale, wanted = gather(
-        features, history, boundary_rows, picks, stale_rows, tile, groups, members
+    tile_src = tile_src.reshape(1, -1)
+    halo, stale, wanted, *plans = gather(
+        features, history, boundary_rows, picks, stale_rows, tile_src, tile, groups, members
     )
     layer_out, row_grad, halo_grad, part = local(
         tile_src, plans, features, halo, stale, tiles, degree, w_self, w_neigh, cotangent

time: 75.1 us -> 71.1 us (0.947)
  other arithmetic: 3.36 us -> 0 us
  between operations: 3.33 us -> 0.66 us
  local copies, waits for them, and re-layouts: 5.96 us -> 7.96 us
    reduce_sum x7 -> x0, other arithmetic: 2.16 us -> none  [the longest x1 0.81 us: plan(): jnp.sum(jnp.where(pos[None, :] == slot[:, None], index[None, :] + 1, 0),...]
    unnamed x11 -> x5, local copies, waits for them, and re-layouts: 5.67 us -> 7.3 us
    select_n x1 -> x0, other arithmetic: 1.18 us -> none  [plan(): quad = jnp.where(first < end, quad, 2 * wanted_sources + 1)]
where the time goes in v4:
time: 71.1 us; the launch traced here: 70.7 us
  Pallas kernels  62.1 us (87%)
  local copies, waits for them, and re-layouts  7.96 us (11%)
    pallas_call x1, Pallas kernels, local(): pl.pallas_call(local_kernel, out_shape=(jax.ShapeDtypeStruct((nodes, widt...  26.5 us
    pallas_call x1, Pallas kernels, combine(): pl.pallas_call(functools.partial(combine_kernel, groups, members, factor)...  18.6 us
    pallas_call x1, Pallas kernels, gather(): pl.pallas_call(functools.partial(gather_kernel, groups, members), out_sha...  17 us
    unnamed x5, local copies, waits for them, and re-layouts  7.3 us

profile of v4, /device:TPU:0, one launch (start us, length us, event | category | flops | bytes accessed | tf_op | source)
XLA Modules:
  0.0 70.7 jit_solution(5256529936303931240)
XLA Ops:
  0.6 1.3 %copy.18.picks = s32[8,1]{1,0:T(8,128)} copy(s32[8,1]{0,1:T(1,128)} %param.17) | data formatting | bytes 64 | tf_op args[6]
  2.0 0.8 %copy.17 = s32[32,16]{1,0:T(8,128)S(1)} copy(s32[32,16]{0,1:T(8,128)} %param.14) | data formatting | bytes 4096 | tf_op args[3]
  2.7 0.7 reshape.14.tile_src.src
  3.4 17.0 %shard_map.138 = (bf16[8,128,128]{2,1,0:T(8,128)(2,1)}, bf16[8,128,128]{2,1,0:T(8,128)(2,1)}, s32[8,1,8,128]{3,2,1,0:T(8,128)}, s32[1,640]{1,0:T(1,128)}, s32[1,256]{1,0:T(1,128)}, /*index=5*/s32[1,128]{1,0:T(1,128)}) custom-call(bf16[4096,128]{1,0:T(8,128)(2,1)} %feats.1, bf16[4096,128]{1,0:T(8,128)(2,1)} %hist_in.1, s32[1,256]{1,0:T(1,128)} %rows.3, ...), custom_call_target="tpu_custom_call" | custom-call | tf_op jit(solution)/shard_map/pallas_call | solution.py:366
  20.4 26.5 %shard_map.139 = (bf16[4096,128]{1,0:T(8,128)(2,1)}, f32[4096,128]{1,0:T(8,128)}, bf16[8,128,128]{2,1,0:T(8,128)(2,1)}, f32[256,128]{1,0:T(8,128)}) custom-call(s32[1,512]{1,0:T(1,128)} %reshape.14.tile_src.src, s32[1,640]{1,0:T(1,128)} %get-tuple-element.17.code, s32[1,256]{1,0:T(1,128)} %get-tuple-element.18.quad, s32[1,128]{1,0:T(1,128)} %get-tuple-element.19.used, ...), custom_call_target="tpu_custom_call" | custom-call | tf_op jit(solution)/shard_map/pallas_call | solution.py:186
  46.9 18.6 %shard_map.140 = (bf16[4096,128]{1,0:T(8,128)(2,1)}, f32[128,128]{1,0:T(8,128)}, f32[128,128]{1,0:T(8,128)}) custom-call(f32[4096,128]{1,0:T(8,128)} %get-tuple-element.23.row_grad_in, bf16[8,128,128]{2,1,0:T(8,128)(2,1)} %get-tuple-element.24.halo_grad, f32[256,128]{1,0:T(8,128)} %get-tuple-element.25.part, s32[8,1,8,128]{3,2,1,0:T(8,128)} %get-tuple-element.26.wanted, ...), custom_call_target="tpu_custom_call" | custom-call | tf_op jit(solution)/shard_map/pallas_call | solution.py:519
  65.5 2.3 %copy.22 = bf16[4096,128]{1,0:T(8,128)(2,1)} copy(bf16[4096,128]{1,0:T(8,128)(2,1)} %get-tuple-element.35) | data formatting | bytes 2097152
  67.8 1.5 %copy.23 = f32[128,128]{1,0:T(8,128)} copy(f32[128,128]{1,0:T(8,128)} %get-tuple-element.36) | data formatting | bytes 131072
  69.2 1.5 %copy.24 = f32[128,128]{1,0:T(8,128)} copy(f32[128,128]{1,0:T(8,128)} %get-tuple-element.37) | data formatting | bytes 131072

commit v5 on v4

--- a/solution.py
+++ b/solution.py
@@ -399,15 +399,13 @@
 def combine_kernel(
     groups,
     members,
-    factor,
     row_grad_in,
     halo_grad,
     part,
     wanted,
     rows,
     grad_features,
-    g_self,
-    g_neigh,
+    grads,
     row_grad,
     l_sem,
     returned,
@@ -503,13 +501,12 @@
     pl.loop(0, nodes // depth)(add)
     for copy in third:
         copy.wait_recv()
-    g_self[...] = whole[:width, :] * factor
-    g_neigh[...] = whole[width:, :] * factor
+    grads[...] = whole[...]
     for copy in first + second + third + copies:
         copy.wait_send()
 
 
-def combine(row_grad, halo_grad, part, wanted, boundary_rows, groups, members, factor):
+def combine(row_grad, halo_grad, part, wanted, boundary_rows, groups, members):
     nodes, width = row_grad.shape
     tile = halo_grad.shape[1]
     taken = wanted.shape[1]
@@ -517,14 +514,13 @@
     vmem = pl.BlockSpec(memory_space=pltpu.VMEM)
     dma = pltpu.SemaphoreType.DMA
     return pl.pallas_call(
-        functools.partial(combine_kernel, groups, members, factor),
+        functools.partial(combine_kernel, groups, members),
         out_shape=(
             jax.ShapeDtypeStruct((nodes, width), BF16),
-            jax.ShapeDtypeStruct((width, part.shape[1]), F32),
-            jax.ShapeDtypeStruct((width, part.shape[1]), F32),
+            jax.ShapeDtypeStruct(part.shape, F32),
         ),
         in_specs=[pl.BlockSpec(memory_space=pl.ANY)] + [vmem] * 4,
-        out_specs=[vmem] * 3,
+        out_specs=[vmem] * 2,
         scratch_shapes=[
             pltpu.VMEM((nodes, width), F32),
             dma(()),
@@ -573,10 +569,11 @@
         tile_src, plans, features, halo, stale, tiles, degree, w_self, w_neigh, cotangent
     )
     factor = 1.0 / math.sqrt(features.shape[0] * members * groups)
-    grad_features, grad_self, grad_neigh = combine(
-        row_grad, halo_grad, part, wanted, boundary_rows, groups, members, factor
-    )
-    return (layer_out, grad_features, grad_self, grad_neigh)
+    grad_features, grads = combine(
+        row_grad, halo_grad, part, wanted, boundary_rows, groups, members
+    )
+    width = features.shape[1]
+    return (layer_out, grad_features, grads[:width] * factor, grads[width:] * factor)
 
 
 def solution(mesh):

time: 71.1 us -> 69.6 us (0.979)
  local copies, waits for them, and re-layouts: 7.96 us -> 5.01 us
  other arithmetic: 0 us -> 1.53 us
    unnamed x5 -> x3, local copies, waits for them, and re-layouts: 7.3 us -> 4.35 us
    mul x0 -> x1, other arithmetic: none -> 1.53 us  [on_device(): grads[width:] * factor]
where the time goes in v5:
time: 69.6 us; the launch traced here: 69.3 us
  Pallas kernels  62.1 us (89%)
  local copies, waits for them, and re-layouts  5.01 us (7%)
  other arithmetic  1.53 us (2%)
    pallas_call x1, Pallas kernels, local(): pl.pallas_call(local_kernel, out_shape=(jax.ShapeDtypeStruct((nodes, widt...  26.1 us
    pallas_call x1, Pallas kernels, combine(): pl.pallas_call(functools.partial(combine_kernel, groups, members), out_sh...  19 us
    pallas_call x1, Pallas kernels, gather(): pl.pallas_call(functools.partial(gather_kernel, groups, members), out_sha...  17 us
    unnamed x3, local copies, waits for them, and re-layouts  4.35 us
    mul x1, other arithmetic, on_device(): grads[width:] * factor  1.53 us

profile of v5, /device:TPU:0, one launch (start us, length us, event | category | flops | bytes accessed | tf_op | source)
XLA Modules:
  0.0 69.3 jit_solution(15114674861312700171)
XLA Ops:
  0.6 1.3 %copy.18.picks = s32[8,1]{1,0:T(8,128)} copy(s32[8,1]{0,1:T(1,128)} %param.17) | data formatting | bytes 64 | tf_op args[6]
  2.0 0.8 %copy.17 = s32[32,16]{1,0:T(8,128)S(1)} copy(s32[32,16]{0,1:T(8,128)} %param.14) | data formatting | bytes 4096 | tf_op args[3]
  2.7 0.7 reshape.14.tile_src.src
  3.4 17.0 %shard_map.138 = (bf16[8,128,128]{2,1,0:T(8,128)(2,1)}, bf16[8,128,128]{2,1,0:T(8,128)(2,1)}, s32[8,1,8,128]{3,2,1,0:T(8,128)}, s32[1,640]{1,0:T(1,128)}, s32[1,256]{1,0:T(1,128)}, /*index=5*/s32[1,128]{1,0:T(1,128)}) custom-call(bf16[4096,128]{1,0:T(8,128)(2,1)} %feats.1, bf16[4096,128]{1,0:T(8,128)(2,1)} %hist_in.1, s32[1,256]{1,0:T(1,128)} %rows.3, ...), custom_call_target="tpu_custom_call" | custom-call | tf_op jit(solution)/shard_map/pallas_call | solution.py:366
  20.4 26.1 %shard_map.139 = (bf16[4096,128]{1,0:T(8,128)(2,1)}, f32[4096,128]{1,0:T(8,128)}, bf16[8,128,128]{2,1,0:T(8,128)(2,1)}, f32[256,128]{1,0:T(8,128)}) custom-call(s32[1,512]{1,0:T(1,128)} %reshape.14.tile_src.src, s32[1,640]{1,0:T(1,128)} %get-tuple-element.16.code, s32[1,256]{1,0:T(1,128)} %get-tuple-element.17.quad, s32[1,128]{1,0:T(1,128)} %get-tuple-element.18.used, ...), custom_call_target="tpu_custom_call" | custom-call | tf_op jit(solution)/shard_map/pallas_call | solution.py:186
  46.4 19.0 %shard_map.140 = (bf16[4096,128]{1,0:T(8,128)(2,1)}, f32[256,128]{1,0:T(8,128)}) custom-call(f32[4096,128]{1,0:T(8,128)} %get-tuple-element.22.row_grad_in, bf16[8,128,128]{2,1,0:T(8,128)(2,1)} %get-tuple-element.23.halo_grad, f32[256,128]{1,0:T(8,128)} %get-tuple-element.24.part, s32[8,1,8,128]{3,2,1,0:T(8,128)} %get-tuple-element.25.wanted, s32[1,256]{1,0:T(1,128)} %rows.3), custom_call_target="tpu_custom_call" | custom-call | tf_op jit(solution)/shard_map/pallas_call | solution.py:516
  65.5 1.5 %slice_multiply_fusion = (f32[128,128]{1,0:T(8,128)}, f32[128,128]{1,0:T(8,128)}) fusion(f32[256,128]{1,0:T(8,128)} %get-tuple-element.27), kind=kLoop, calls=%fused_computation | loop fusion | flops 32768 | bytes 262144 | tf_op jit(solution)/shard_map/mul | solution.py:576
  67.0 2.3 %copy.20 = bf16[4096,128]{1,0:T(8,128)(2,1)} copy(bf16[4096,128]{1,0:T(8,128)(2,1)} %get-tuple-element.35) | data formatting | bytes 2097152
